TPU v7x, 32 devices: a whole 2x2x4 slice. The times are simulated.
32 devices in a mesh: groups: 2 (over x), dp: 16 (over z, y, core).
Axes of the slice: x: 2, y: 2, z: 4, core: 2. Of those that a mesh axis runs over, the one named last changes fastest.
Arguments:
- images: bfloat16 [16, 128, 128, 320], P('groups', 'dp'), parts along dimension 0, may hold values from -6 to 6
- kernel_weights: bfloat16 [16, 2, 3, 3, 320, 320], P('dp'), may hold values from -0.109375 to 0.109375
- kernel_momentum: float32 [16, 2, 3, 3, 320, 320], P('dp'), may hold values from -0.12 to 0.12
- kernel_grads: bfloat16 [16, 2, 3, 3, 320, 320], P('dp'), may hold values from -0.119628906 to 0.119628906
- owners: int32 [2], replicated, may hold values from 0 to 15
Outputs:
- blocks_out: bfloat16 [16, 128, 128, 320], P('groups', 'dp'), parts along dimension 0
There are 2 independent parts, one for each index of `groups`. A program takes and returns all parts, laid end to end along the dimension named above; an argument that names none is the same for every part. Nothing has to cross between parts.
Inputs may be any that keep to these rules, and one draw needn't show every extreme that they name: `owners`: each entry is a slot index along the first dimension of the kernel state.
All inputs are finite; a program needn't handle non-finite values.
Results may differ from a plain program's by a relative error of at most 0.0095.
Values may be sent and summed in bfloat16 or wider, within the bound.
A program may use at most 128 MiB of HBM per device.

v0:
```python
import jax
import jax.numpy as jnp
from jax import lax
from jax.sharding import PartitionSpec as P

momentum_decay = 0.9
learn_rate = 0.5


def from_root(x, axis, root):
    mine = lax.axis_index(axis) == root
    return lax.psum(jnp.where(mine, x, jnp.zeros_like(x)), axis)


def padded(cells, sides, width):
    for axis, dim in sides:
        count = lax.axis_size(axis)
        ends = count - 1
        head = lax.slice_in_dim(cells, 0, width, axis=dim)
        tail = lax.slice_in_dim(cells, cells.shape[dim] - width, cells.shape[dim], axis=dim)
        cells = jnp.concatenate(
            [
                lax.ppermute(tail, axis, [(i, (i + 1) % count) for i in range(ends)]),
                cells,
                lax.ppermute(head, axis, [((i + 1) % count, i) for i in range(ends)]),
            ],
            axis=dim,
        )
    return cells


def conv_rows(activated, kernel):
    return lax.conv_general_dilated(
        activated,
        kernel,
        (1, 1),
        ((0, 0), (1, 1)),
        dimension_numbers=("NHWC", "HWIO", "NHWC"),
        preferred_element_type=jnp.float32,
    )


def renew(kernel_weights, kernel_momentum, kernel_grads, owners, kernel_index):
    velocity = momentum_decay * kernel_momentum[0, kernel_index] + kernel_grads[
        0, kernel_index
    ].astype(jnp.float32)
    updated = (kernel_weights[0, kernel_index].astype(jnp.float32) - learn_rate * velocity).astype(
        jnp.bfloat16
    )
    return from_root(updated, "dp", owners[kernel_index])


def residual_conv(strip_field, kernel):
    activated = jax.nn.silu(strip_field.astype(jnp.float32)).astype(jnp.bfloat16)
    with_rims = padded(activated, (("dp", 1),), 1)
    branch = conv_rows(with_rims, kernel)
    return strip_field.astype(jnp.float32) + branch


def local(images, kernel_weights, kernel_momentum, kernel_grads, owners):
    first_kernel = renew(kernel_weights, kernel_momentum, kernel_grads, owners, 0)
    hidden = residual_conv(images, first_kernel).astype(jnp.bfloat16)
    second_kernel = renew(kernel_weights, kernel_momentum, kernel_grads, owners, 1)
    return residual_conv(hidden, second_kernel).astype(jnp.bfloat16)


def solution(mesh):
    placed = (
        P("groups", "dp", None, None),
        P("dp", None, None, None, None, None),
        P("dp", None, None, None, None, None),
        P("dp", None, None, None, None, None),
        P(),
    )
    return jax.shard_map(
        local, mesh=mesh, in_specs=placed, out_specs=P("groups", "dp", None, None), check_vma=False
    )
```

profile of v0, /device:TPU:1, one launch (start us, length us, event | category | flops | bytes accessed | tf_op | source)
XLA Modules:
  0.0 239.2 jit_solution(6173910143435806145)
XLA Ops:
  6.5 0.0 all-reduce.3.cloned.1.call-start
  6.5 1.3 fusion.34
  9.1 9.4 %fusion.29 = (bf16[3,3,320,320]{3,2,1,0:T(8,128)(2,1)}, bf16[3,3,320,320]{3,2,1,0:T(8,128)(2,1)}) fusion(f32[1,2,3,3,320,320]{5,4,3,2,1,0:T(8,128)} %param.7, bf16[1,2,3,3,320,320]{5,4,3,2,1,0:T(8,128)(2,1)} %param.8, bf16[1,2,3,3,320,320]{5,4,3,2,1,0:T(8,128)(2,1)} %param.6, pred[]{:T(512)S(6)} %eq.7, pred[]{:T(512)S(6)} %eq.6), kind=kLoop, calls=%fused_computation.33 | loop fusion | flops 14745600 | bytes 18432002 | tf_op jit(solution)/shard_map/jit(_where)/select_n | solution.py:12
  18.5 0.0 all-reduce.3.cloned.1.call-update
  18.5 8.6 %copy.8 = bf16[8,8,128,320]{3,0,2,1:T(8,128)(2,1)} copy(bf16[8,8,128,320]{2,3,1,0:T(8,128)(2,1)} %param.5) | data formatting | bytes 10485760 | tf_op args[0]
  27.1 5.5 %fusion.3 = bf16[8,8,128,320]{3,0,2,1:T(8,128)(2,1)S(1)} fusion(bf16[8,8,128,320]{3,0,2,1:T(8,128)(2,1)} %copy.8), kind=kLoop, calls=%fused_computation.9 | loop fusion | flops 15728640 | bytes 10485760 | tf_op jit(solution)/shard_map/convert_element_type | solution.py:54
  32.6 0.0 copy-start
  32.6 2.6 %copy-done = bf16[8,8,128,320]{3,0,2,1:T(8,128)(2,1)} copy-done((bf16[8,8,128,320]{3,0,2,1:T(8,128)(2,1)}, bf16[8,8,128,320]{3,0,2,1:T(8,128)(2,1)S(1)}, u32[]{:S(2)}) %copy-start) | copy-done | bytes 5242904
  35.2 0.2 fusion.33
  35.4 0.5 copy.10
  35.9 1.9 collective-permute-start.1
  37.9 0.5 copy.9
  38.4 4.9 %collective-permute-start = (bf16[8,1,128,320]{2,3,1,0:T(8,128)(2,1)S(1)}, bf16[8,1,128,320]{2,3,1,0:T(8,128)(2,1)S(1)}, u32[]{:S(2)}, u32[]{:S(2)}) collective-permute-start(bf16[8,1,128,320]{2,3,1,0:T(8,128)(2,1)S(1)} %copy.9), channel_id=1, source_target_pairs={{0,1},{1,2},{2,3},{3,4},{4,5},{5,6},{6,7},{7,8},{8,9},{9,10},{10,1... | collective-permute-start | bytes 1966088 | tf_op jit(solution)/shard_map/ppermute | solution.py:23
  43.3 8.2 %collective-permute-done.1 = bf16[8,1,128,320]{2,3,1,0:T(8,128)(2,1)S(1)} collective-permute-done((bf16[8,1,128,320]{2,3,1,0:T(8,128)(2,1)S(1)}, bf16[8,1,128,320]{2,3,1,0:T(8,128)(2,1)S(1)}, u32[]{:S(2)}, u32[]{:S(2)}) %collective-permute-start.1) | collective-permute-done | bytes 655392 | tf_op jit(solution)/shard_map/ppermute | solution.py:25
  51.5 0.5 copy.12
  52.1 2.1 collective-permute-done
  54.2 0.5 copy.11
  54.7 83.4 %all-reduce.3.cloned.1.call-done = (bf16[3,3,320,320]{3,2,1,0:T(8,128)(2,1)}, bf16[3,3,320,320]{3,2,1,0:T(8,128)(2,1)}) async-done(((bf16[3,3,320,320]{3,2,1,0:T(8,128)(2,1)}, bf16[3,3,320,320]{3,2,1,0:T(8,128)(2,1)}), (bf16[3,3,320,320]{3,2,1,0:T(8,128)(2,1)}, bf16[3,3,320,320]{3,2,1,0:T(8,128)(2,1)})) %all-reduce.3.cloned.1.call-update) | async-done | bytes 3686416 | tf_op jit(solution)/shard_map/psum | solution.py:12
  138.1 32.1 %fusion.8 = (bf16[8,8,128,320]{3,0,2,1:T(8,128)(2,1)S(1)}, bf16[8,8,128,320]{3,0,2,1:T(8,128)(2,1)}) fusion(bf16[3,3,320,320]{3,2,1,0:T(8,128)(2,1)} %get-tuple-element.5, bf16[8,1,128,320]{3,0,2,1:T(8,128)(2,1)S(1)} %copy.12, bf16[8,8,128,320]{3,0,2,1:T(8,128)(2,1)} %copy-done, bf16[8,1,128,320]{3,0,2,1:T(8,128)(2,1)S(1)} %copy.11, ...), kind=kOutput, calls=%fused_computation.14 | convolution fusion | flops 15064104960 | bytes 24125440 | tf_op jit(solution)/shard_map/conv_general_dilated | solution.py:33
  170.2 0.0 copy-start.1
  170.2 0.2 fusion.32
  170.4 2.5 %copy-done.1 = bf16[8,8,128,320]{3,0,2,1:T(8,128)(2,1)} copy-done((bf16[8,8,128,320]{3,0,2,1:T(8,128)(2,1)}, bf16[8,8,128,320]{3,0,2,1:T(8,128)(2,1)S(1)}, u32[]{:S(2)}) %copy-start.1) | copy-done | bytes 5242904
  172.9 0.5 copy.14
  173.4 4.4 %collective-permute-start.3 = (bf16[8,1,128,320]{2,3,1,0:T(8,128)(2,1)S(1)}, bf16[8,1,128,320]{2,3,1,0:T(8,128)(2,1)S(1)}, u32[]{:S(2)}, u32[]{:S(2)}) collective-permute-start(bf16[8,1,128,320]{2,3,1,0:T(8,128)(2,1)S(1)} %copy.14), channel_id=1, source_target_pairs={{1,0},{2,1},{3,2},{4,3},{5,4},{6,5},{7,6},{8,7},{9,8},{10,9},{11,1... | collective-permute-start | bytes 1966088 | tf_op jit(solution)/shard_map/ppermute | solution.py:25
  177.8 0.5 copy.13
  178.3 2.7 %collective-permute-start.2 = (bf16[8,1,128,320]{2,3,1,0:T(8,128)(2,1)S(1)}, bf16[8,1,128,320]{2,3,1,0:T(8,128)(2,1)S(1)}, u32[]{:S(2)}, u32[]{:S(2)}) collective-permute-start(bf16[8,1,128,320]{2,3,1,0:T(8,128)(2,1)S(1)} %copy.13), channel_id=1, source_target_pairs={{0,1},{1,2},{2,3},{3,4},{4,5},{5,6},{6,7},{7,8},{8,9},{9,10},{10,1... | collective-permute-start | bytes 1966088 | tf_op jit(solution)/shard_map/ppermute | solution.py:23
  181.1 5.6 %collective-permute-done.3 = bf16[8,1,128,320]{2,3,1,0:T(8,128)(2,1)S(1)} collective-permute-done((bf16[8,1,128,320]{2,3,1,0:T(8,128)(2,1)S(1)}, bf16[8,1,128,320]{2,3,1,0:T(8,128)(2,1)S(1)}, u32[]{:S(2)}, u32[]{:S(2)}) %collective-permute-start.3) | collective-permute-done | bytes 655392 | tf_op jit(solution)/shard_map/ppermute | solution.py:25
  186.7 0.5 copy.16
  187.2 5.9 %collective-permute-done.2 = bf16[8,1,128,320]{2,3,1,0:T(8,128)(2,1)S(1)} collective-permute-done((bf16[8,1,128,320]{2,3,1,0:T(8,128)(2,1)S(1)}, bf16[8,1,128,320]{2,3,1,0:T(8,128)(2,1)S(1)}, u32[]{:S(2)}, u32[]{:S(2)}) %collective-permute-start.2) | collective-permute-done | bytes 655392 | tf_op jit(solution)/shard_map/ppermute | solution.py:23
  193.1 0.5 copy.15
  193.7 30.2 %fusion.9 = bf16[8,8,128,320]{3,0,2,1:T(8,128)(2,1)} fusion(bf16[8,8,128,320]{3,0,2,1:T(8,128)(2,1)} %get-tuple-element.16, bf16[3,3,320,320]{3,2,1,0:T(8,128)(2,1)} %get-tuple-element.6, bf16[8,1,128,320]{3,0,2,1:T(8,128)(2,1)S(1)} %copy.16, bf16[8,8,128,320]{3,0,2,1:T(8,128)(2,1)} %copy-done.1, bf16[8,1,128,320]{3,0,2,1:T(8,128)(2,1)S(1)} %copy.15), kind=kOutput, calls=%fused_computation.15 | convolution fusion | flops 15048376320 | bytes 18882560 | tf_op jit(solution)/shard_map/conv_general_dilated | solution.py:33
  223.8 8.5 %copy.17 = bf16[8,8,128,320]{2,3,1,0:T(8,128)(2,1)} copy(bf16[8,8,128,320]{3,0,2,1:T(8,128)(2,1)} %fusion.9) | data formatting | bytes 10485760 | tf_op jit(solution)/shard_map/convert_element_type | solution.py:64
Async XLA Ops:
  6.5 131.6 %all-reduce.3.cloned.1.call-start = ((), (), s32[]{:S(2)}) async-start(), calls=%async_computation | async-start | bytes 8847360 | tf_op jit(solution)/shard_map/psum | solution.py:12
  32.6 2.6 %copy-start = (bf16[8,8,128,320]{3,0,2,1:T(8,128)(2,1)}, bf16[8,8,128,320]{3,0,2,1:T(8,128)(2,1)S(1)}, u32[]{:S(2)}) copy-start(bf16[8,8,128,320]{3,0,2,1:T(8,128)(2,1)S(1)} %fusion.3) | copy-start | bytes 15728644
  35.9 15.6 %collective-permute-start.1 = (bf16[8,1,128,320]{2,3,1,0:T(8,128)(2,1)S(1)}, bf16[8,1,128,320]{2,3,1,0:T(8,128)(2,1)S(1)}, u32[]{:S(2)}, u32[]{:S(2)}) collective-permute-start(bf16[8,1,128,320]{2,3,1,0:T(8,128)(2,1)S(1)} %copy.10), channel_id=1, source_target_pairs={{1,0},{2,1},{3,2},{4,3},{5,4},{6,5},{7,6},{8,7},{9,8},{10,9},{11,1... | collective-permute-start | bytes 1966088 | tf_op jit(solution)/shard_map/ppermute | solution.py:25
  38.4 15.8 %collective-permute-start = (bf16[8,1,128,320]{2,3,1,0:T(8,128)(2,1)S(1)}, bf16[8,1,128,320]{2,3,1,0:T(8,128)(2,1)S(1)}, u32[]{:S(2)}, u32[]{:S(2)}) collective-permute-start(bf16[8,1,128,320]{2,3,1,0:T(8,128)(2,1)S(1)} %copy.9), channel_id=1, source_target_pairs={{0,1},{1,2},{2,3},{3,4},{4,5},{5,6},{6,7},{7,8},{8,9},{9,10},{10,1... | collective-permute-start | bytes 1966088 | tf_op jit(solution)/shard_map/ppermute | solution.py:23
  170.2 2.6 %copy-start.1 = (bf16[8,8,128,320]{3,0,2,1:T(8,128)(2,1)}, bf16[8,8,128,320]{3,0,2,1:T(8,128)(2,1)S(1)}, u32[]{:S(2)}) copy-start(bf16[8,8,128,320]{3,0,2,1:T(8,128)(2,1)S(1)} %get-tuple-element.15) | copy-start | bytes 15728644
  173.4 13.3 %collective-permute-start.3 = (bf16[8,1,128,320]{2,3,1,0:T(8,128)(2,1)S(1)}, bf16[8,1,128,320]{2,3,1,0:T(8,128)(2,1)S(1)}, u32[]{:S(2)}, u32[]{:S(2)}) collective-permute-start(bf16[8,1,128,320]{2,3,1,0:T(8,128)(2,1)S(1)} %copy.14), channel_id=1, source_target_pairs={{1,0},{2,1},{3,2},{4,3},{5,4},{6,5},{7,6},{8,7},{9,8},{10,9},{11,1... | collective-permute-start | bytes 1966088 | tf_op jit(solution)/shard_map/ppermute | solution.py:25
  178.3 14.8 %collective-permute-start.2 = (bf16[8,1,128,320]{2,3,1,0:T(8,128)(2,1)S(1)}, bf16[8,1,128,320]{2,3,1,0:T(8,128)(2,1)S(1)}, u32[]{:S(2)}, u32[]{:S(2)}) collective-permute-start(bf16[8,1,128,320]{2,3,1,0:T(8,128)(2,1)S(1)} %copy.13), channel_id=1, source_target_pairs={{0,1},{1,2},{2,3},{3,4},{4,5},{5,6},{6,7},{7,8},{8,9},{9,10},{10,1... | collective-permute-start | bytes 1966088 | tf_op jit(solution)/shard_map/ppermute | solution.py:23
Sparse Core Ops, SparseCore 0:
  18.6 119.4 all-reduce.2
where the time goes:
time: 240 us; the launch traced here: 239 us
  waiting for transfers between devices  105 us (44%)
  matrix products  62.2 us (26%)
  local copies, waits for them, and re-layouts  28.2 us (12%)
  other arithmetic  14.8 us (6%)
  between operations  14.7 us (6%)
  starting transfers between devices  13.9 us (6%)
    psum x1, waiting for transfers between devices, from_root(): return lax.psum(jnp.where(mine, x, jnp.zeros_like(x)), axis)  83.4 us
    conv_general_dilated x2, matrix products, conv_rows(): lax.conv_general_dilated(activated, kernel, (1, 1), ((0, 0), (1, 1)), dim...  62.2 us
    ppermute x2, waiting for transfers between devices, padded(): lax.ppermute(head, axis, [((i + 1) % count, i) for i in range(ends)])  13.8 us
    unnamed x5, local copies, waits for them, and re-layouts  13.8 us
    select_n x1, other arithmetic, from_root(): return lax.psum(jnp.where(mine, x, jnp.zeros_like(x)), axis)  9.39 us
    convert_element_type x1, local copies, waits for them, and re-layouts, local(): return residual_conv(hidden, second_kernel).astype(jnp.bfloat16)  8.51 us
    ppermute x2, waiting for transfers between devices, padded(): lax.ppermute(tail, axis, [(i, (i + 1) % count) for i in range(ends)])  8.02 us
    ppermute x2, starting transfers between devices, padded(): lax.ppermute(tail, axis, [(i, (i + 1) % count) for i in range(ends)])  7.59 us
  transfers between devices with their start and end apart: 5, of which 5 were waited for; matrix products, arithmetic and copies ran while one was open for 7% of the time, Pallas kernels for 0%

commit v1 on v0

v1 whole, which is shorter than its diff:
```python
import functools

import jax
import jax.numpy as jnp
from jax import lax
from jax.experimental import pallas as pl
from jax.experimental.pallas import tpu as pltpu
from jax.sharding import PartitionSpec as P

momentum_decay = 0.9
learn_rate = 0.5
MESH = pl.DeviceIdType.MESH
hop = 2


def spread_kernel(
    groups, depth, chunks, mask_ref, w_hbm, m_hbm, g_hbm, out_ref,
    w_buf, m_buf, g_buf, own, pair_out, pair_in, col, col_in, joined, fwd, fwd_in, back, back_in,
    load_sem, pair_sem, col_sem, fwd_sem, back_sem, mate_sem, cross_sem, pass_sem,
):
    group, at = lax.axis_index("groups"), lax.axis_index("dp")
    z, y, core = at // 4, (at // 2) % 2, at % 2
    mate = at + 1 - 2 * core
    across = at + 2 - 4 * y
    share = 2 * group + core
    last = depth - 1

    def loads(k):
        src = pl.ds(2 * group, 2)
        return [
            pltpu.make_async_copy(ref.at[k, src], buf.at[k], load_sem.at[i, k])
            for i, (ref, buf) in enumerate(((w_hbm, w_buf), (m_hbm, m_buf), (g_hbm, g_buf)))
        ]

    def remote(src, dst, sem, k, **where):
        return pltpu.make_async_remote_copy(
            src, dst, sem.at[0, k], sem.at[1, k], device_id=where, device_id_type=MESH
        )

    def to_pair(k):
        return remote(pair_out.at[k], pair_in.at[k], pair_sem, k, dp=mate)

    def to_col(k):
        return remote(col.at[k], col_in.at[k], col_sem, k, dp=across)

    def to_fwd(k, up=4):
        return remote(fwd.at[k], fwd_in.at[k], fwd_sem, k, dp=at + up)

    def to_back(k, down=4):
        return remote(back.at[k], back_in.at[k], back_sem, k, dp=at - down)

    def to_mate(k):
        return remote(out_ref.at[k, share], out_ref.at[k, share], mate_sem, k, dp=mate)

    others = [lax.rem(group + step, groups) for step in range(1, groups)]

    def to_cross(k, i):
        return remote(
            out_ref.at[k, share], out_ref.at[k, share], cross_sem.at[i], k, groups=others[i]
        )

    def from_cross(k, i):
        sent_by = lax.rem(group + groups - 1 - i, groups)
        slot = 2 * sent_by + core
        return pltpu.make_async_remote_copy(
            out_ref.at[k, slot], out_ref.at[k, slot], cross_sem.at[i, 0, k], cross_sem.at[i, 1, k],
            device_id={"groups": others[i]}, device_id_type=MESH,
        )

    def to_pass(k, i):
        slot = 2 * lax.rem(group + groups - 1 - i, groups) + core
        return remote(out_ref.at[k, slot], out_ref.at[k, slot], pass_sem.at[i], k, dp=mate)

    def start_loads(k, carry):
        for copy in loads(k):
            copy.start()
        return carry

    lax.fori_loop(0, chunks, start_loads, 0)

    barrier = pltpu.get_barrier_semaphore()
    pl.semaphore_signal(barrier, inc=1, device_id={"dp": mate}, device_id_type=MESH)
    pl.semaphore_signal(barrier, inc=1, device_id={"dp": across}, device_id_type=MESH)
    for other in others:
        pl.semaphore_signal(barrier, inc=1, device_id={"groups": other}, device_id_type=MESH)

    @pl.when(z > 0)
    def _():
        pl.semaphore_signal(barrier, inc=1, device_id={"dp": at - 4}, device_id_type=MESH)

    @pl.when(z < last)
    def _():
        pl.semaphore_signal(barrier, inc=1, device_id={"dp": at + 4}, device_id_type=MESH)

    ahead, behind = jnp.where(z < last, 1, 0), jnp.where(z > 0, 1, 0)
    pl.semaphore_wait(barrier, 1 + groups + ahead + behind)

    def at_step(k, what):
        pl.when((k >= 0) & (k < chunks))(lambda: what(k))

    def renew(k):
        for copy in loads(k):
            copy.wait()
        mine = mask_ref[k] > 0.5

        def new(c):
            velocity = momentum_decay * m_buf[k, c] + g_buf[k, c].astype(jnp.float32)
            updated = w_buf[k, c].astype(jnp.float32) - learn_rate * velocity
            return jnp.where(mine, updated, 0.0).astype(jnp.bfloat16)

        pair_out[k] = new(1 - core)
        to_pair(k).start()
        own[k] = new(core)

    def join_pair(k):
        to_pair(k).wait_recv()
        col[k] = own[k] + pair_in[k]
        to_col(k).start()

    def join_col(k):
        to_col(k).wait_recv()
        joined[k] = col[k] + col_in[k]

    def go_fwd(k):
        @pl.when(z == 0)
        def _():
            fwd[k] = joined[k]

        @pl.when(z > 0)
        def _():
            to_fwd(k, -4).wait_recv()
            fwd[k] = joined[k] + fwd_in[k]

        @pl.when(z < last)
        def _():
            to_fwd(k).start()

    def go_back(k):
        @pl.when(z == last)
        def _():
            back[k] = joined[k]

        @pl.when(z < last)
        def _():
            to_back(k, -4).wait_recv()
            back[k] = joined[k] + back_in[k]

        @pl.when(z > 0)
        def _():
            to_back(k).start()

    def finish(k):
        @pl.when(z < last)
        def _():
            out_ref[k, share] = fwd[k] + back_in[k]

        @pl.when(z == last)
        def _():
            out_ref[k, share] = fwd[k]

        to_mate(k).start()
        for i in range(groups - 1):
            to_cross(k, i).start()

    def pass_on(k):
        for i in range(groups - 1):
            from_cross(k, i).wait_recv()
            to_pass(k, i).start()

    def step(t, carry):
        at_step(t, renew)
        at_step(t - 1, join_pair)
        begin = 1 + hop
        at_step(t - begin, join_col)
        at_step(t - begin - z * hop, go_fwd)
        at_step(t - begin - (last - z) * hop, go_back)
        at_step(t - begin - last * hop, finish)
        at_step(t - begin - last * hop - hop, pass_on)
        return carry

    lax.fori_loop(0, chunks + 1 + hop + last * hop + hop, step, 0)

    def drain(k, carry):
        to_pair(k).wait_send()
        to_col(k).wait_send()

        @pl.when(z < last)
        def _():
            to_fwd(k).wait_send()

        @pl.when(z > 0)
        def _():
            to_back(k).wait_send()

        to_mate(k).wait()
        for i in range(groups - 1):
            to_cross(k, i).wait_send()
            to_pass(k, i).wait()
        return carry

    lax.fori_loop(0, chunks, drain, 0)


def spread(kernel_weights, kernel_momentum, kernel_grads, owners):
    groups, dp = lax.axis_size("groups"), lax.axis_size("dp")
    _, kernels, rows, columns, fan_in, fan_out = kernel_weights.shape
    chunks, shares = kernels * rows * columns, 2 * groups
    part = fan_in // shares
    cut = lambda a: a.reshape(chunks, shares, part, fan_out)
    mine = (owners == lax.axis_index("dp")).astype(jnp.float32)
    mask = jnp.broadcast_to(
        jnp.repeat(mine, rows * columns)[:, None, None], (chunks, 1, fan_out)
    )
    piece = pltpu.VMEM((chunks, part, fan_out), jnp.bfloat16)
    load = lambda dtype: pltpu.VMEM((chunks, 2, part, fan_out), dtype)
    sems = pltpu.SemaphoreType.DMA((2, chunks))
    many = pltpu.SemaphoreType.DMA((groups - 1, 2, chunks))
    out = pl.pallas_call(
        functools.partial(spread_kernel, groups, dp // 4, chunks),
        out_shape=jax.ShapeDtypeStruct((chunks, shares, part, fan_out), jnp.bfloat16),
        in_specs=[pl.BlockSpec(memory_space=pltpu.VMEM)] + [pl.BlockSpec(memory_space=pl.ANY)] * 3,
        out_specs=pl.BlockSpec(memory_space=pltpu.VMEM),
        scratch_shapes=[load(jnp.bfloat16), load(jnp.float32), load(jnp.bfloat16)]
        + [piece] * 10
        + [pltpu.SemaphoreType.DMA((3, chunks)), sems, sems, sems, sems, sems, many, many],
        compiler_params=pltpu.CompilerParams(
            collective_id=0, has_side_effects=True, vmem_limit_bytes=56 << 20
        ),
    )(mask, cut(kernel_weights), cut(kernel_momentum), cut(kernel_grads))
    return out.reshape(kernels, rows, columns, fan_in, fan_out)


def silu(v):
    return v / (1.0 + jnp.exp(-v))


def conv_kernel(x_ref, top_ref, bottom_ref, k_ref, o_ref, patch, wide, rest):
    height, width, channels = x_ref.shape[1:]
    full = channels // 128 // 2 * 256
    tail = channels - full
    reach = 3 * channels
    span = patch.shape[-1]

    @pl.when(pl.program_id(0) == 0)
    def _():
        patch[:, :, reach:] = jnp.zeros((height + 2, width, span - reach), jnp.bfloat16)
        rest[reach:, :] = jnp.zeros((span - reach, rest.shape[1]), jnp.bfloat16)
        for dr in range(3):
            base = dr * span
            wide[base + reach : base + span, :] = jnp.zeros((span - reach, full), jnp.bfloat16)
            for dc in range(3):
                low, high = dc * full, 3 * full + dc * tail
                lanes = slice(dr * tail, (dr + 1) * tail)
                wide[base + low : base + low + full, :] = k_ref[dr, dc, :full, :full]
                wide[base + high : base + high + tail, :] = k_ref[dr, dc, full:, :full]
                rest[low : low + full, lanes] = k_ref[dr, dc, :full, full:]
                rest[high : high + tail, lanes] = k_ref[dr, dc, full:, full:]

    column = lax.broadcasted_iota(jnp.int32, (width, 1), 0)
    for row in range(height + 2):
        if row == 0:
            v = top_ref[0, 0]
        elif row == height + 1:
            v = bottom_ref[0, 0]
        else:
            v = x_ref[0, row - 1]
        a = silu(v.astype(jnp.float32))
        before = jnp.where(column == 0, 0.0, pltpu.roll(a, 1, 0)).astype(jnp.bfloat16)
        after = jnp.where(column == width - 1, 0.0, pltpu.roll(a, width - 1, 0)).astype(jnp.bfloat16)
        for dc, part in enumerate((before, a.astype(jnp.bfloat16), after)):
            patch[row, :, dc * full : (dc + 1) * full] = part[:, :full]
            high = 3 * full + dc * tail
            patch[row, :, high : high + tail] = part[:, full:]

    cells = height * width
    lhs = jnp.concatenate(
        [patch[dr : dr + height].reshape(cells, span) for dr in range(3)], axis=-1
    )
    main = jnp.dot(lhs, wide[...], preferred_element_type=jnp.float32)
    side = jnp.dot(
        patch[...].reshape((height + 2) * width, span), rest[...], preferred_element_type=jnp.float32
    )
    side = (
        side[:cells, :tail]
        + side[width : width + cells, tail : 2 * tail]
        + side[2 * width : 2 * width + cells, 2 * tail : 3 * tail]
    )
    x = x_ref[0].reshape(cells, channels)
    o_ref[0, :, :, :full] = (
        (x[:, :full].astype(jnp.float32) + main).astype(o_ref.dtype).reshape(height, width, full)
    )
    o_ref[0, :, :, full:] = (
        (x[:, full:].astype(jnp.float32) + side).astype(o_ref.dtype).reshape(height, width, tail)
    )


def residual_conv(x, kernel):
    images, height, width, channels = x.shape
    count = lax.axis_size("dp")
    top = lax.ppermute(x[:, -1:], "dp", [(i, i + 1) for i in range(count - 1)])
    bottom = lax.ppermute(x[:, :1], "dp", [(i + 1, i) for i in range(count - 1)])
    full = channels // 128 // 2 * 256
    tail = channels - full
    span = -(-3 * channels // 256) * 256
    image = pl.BlockSpec((1, height, width, channels), lambda i: (i, 0, 0, 0))
    edge = pl.BlockSpec((1, 1, width, channels), lambda i: (i, 0, 0, 0))
    return pl.pallas_call(
        conv_kernel,
        out_shape=jax.ShapeDtypeStruct(x.shape, x.dtype),
        grid=(images,),
        in_specs=[image, edge, edge, pl.BlockSpec(kernel.shape, lambda i: (0, 0, 0, 0))],
        out_specs=image,
        scratch_shapes=[
            pltpu.VMEM((height + 2, width, span), jnp.bfloat16),
            pltpu.VMEM((3 * span, full), jnp.bfloat16),
            pltpu.VMEM((span, 3 * tail), jnp.bfloat16),
        ],
        compiler_params=pltpu.CompilerParams(vmem_limit_bytes=56 << 20),
    )(x, top, bottom, kernel)


def local(images, kernel_weights, kernel_momentum, kernel_grads, owners):
    kernels = spread(kernel_weights, kernel_momentum, kernel_grads, owners)
    hidden = residual_conv(images, kernels[0])
    return residual_conv(hidden, kernels[1])


def solution(mesh):
    placed = (
        P("groups", "dp", None, None),
        P("dp", None, None, None, None, None),
        P("dp", None, None, None, None, None),
        P("dp", None, None, None, None, None),
        P(),
    )
    return jax.shard_map(
        local, mesh=mesh, in_specs=placed, out_specs=P("groups", "dp", None, None), check_vma=False
    )
```

time: 240 us -> 161 us (0.67)
  Pallas kernels: 0 us -> 107 us
  waiting for transfers between devices: 105 us -> 12.2 us
  matrix products: 62.2 us -> 0 us
  other arithmetic: 14.8 us -> 0.01 us
  between operations: 14.7 us -> 0.08 us
  starting transfers between devices: 13.9 us -> 11 us
    pallas_call x0 -> x3, Pallas kernels: none -> 107 us  [the longest x1 54.7 us: spread(): pl.pallas_call(functools.partial(spread_kernel, groups, dp // 4, chunks),...]
    psum x1 -> x0, waiting for transfers between devices: 83.4 us -> none  [from_root(): return lax.psum(jnp.where(mine, x, jnp.zeros_like(x)), axis)]
    conv_general_dilated x2 -> x0, matrix products: 62.2 us -> none  [conv_rows(): lax.conv_general_dilated(activated, kernel, (1, 1), ((0, 0), (1, 1)), dim...]
    ppermute x4, waiting for transfers between devices: 21.8 us -> 12.2 us  [the longest x2 12.2 us: residual_conv(): top = lax.ppermute(x[:, -1:], 'dp', [(i, i + 1) for i in range(count - 1)])]
    select_n x1 -> x0, other arithmetic: 9.39 us -> none  [from_root(): return lax.psum(jnp.where(mine, x, jnp.zeros_like(x)), axis)]
    convert_element_type x1 -> x0, local copies, waits for them, and re-layouts: 8.51 us -> none  [local(): return residual_conv(hidden, second_kernel).astype(jnp.bfloat16)]
    pallas_call x0 -> x1, local copies, waits for them, and re-layouts: none -> 8.19 us  [residual_conv(): pl.pallas_call(conv_kernel, out_shape=jax.ShapeDtypeStruct(x.shape, x.dty...]
    unnamed x5 -> x3, local copies, waits for them, and re-layouts: 13.8 us -> 8.19 us
  transfers between devices with their start and end apart: 5 -> 4, of which waited for: 5 -> 1; matrix products, arithmetic and copies ran while one was open for 7% -> 10% of each run, Pallas kernels for 0% -> 34%
where the time goes in v1:
time: 161 us
  Pallas kernels  107 us (66%)
  local copies, waits for them, and re-layouts  30.5 us (19%)
  waiting for transfers between devices  12.2 us (8%)
  starting transfers between devices  11 us (7%)
    pallas_call x1, Pallas kernels, spread(): pl.pallas_call(functools.partial(spread_kernel, groups, dp // 4, chunks),...  54.7 us
    pallas_call x2, Pallas kernels, residual_conv(): pl.pallas_call(conv_kernel, out_shape=jax.ShapeDtypeStruct(x.shape, x.dty...  52.1 us
    ppermute x2, waiting for transfers between devices, residual_conv(): top = lax.ppermute(x[:, -1:], 'dp', [(i, i + 1) for i in range(count - 1)])  12.2 us
    pallas_call x1, local copies, waits for them, and re-layouts, residual_conv(): pl.pallas_call(conv_kernel, out_shape=jax.ShapeDtypeStruct(x.shape, x.dty...  8.19 us
    unnamed x3, local copies, waits for them, and re-layouts  8.19 us
    ppermute x2, starting transfers between devices, residual_conv(): top = lax.ppermute(x[:, -1:], 'dp', [(i, i + 1) for i in range(count - 1)])  7.18 us
    slice x1, local copies, waits for them, and re-layouts, local(): return residual_conv(hidden, kernels[1])  4.83 us
    ppermute x2, starting transfers between devices, residual_conv(): lax.ppermute(x[:, :1], 'dp', [(i + 1, i) for i in range(count - 1)])  3.85 us
  transfers between devices with their start and end apart: 4, of which 1 were waited for; matrix products, arithmetic and copies ran while one was open for 10% of the time, Pallas kernels for 34%

profile of v1, /device:TPU:1, one launch (start us, length us, event | category | flops | bytes accessed | tf_op | source)
XLA Modules:
  0.0 160.6 jit_solution(17342969889932387403)
XLA Ops:
  0.0 1.4 fusion.1
  1.4 1.9 %collective-permute-start.1 = (bf16[8,1,128,320]{2,3,1,0:T(8,128)(2,1)S(1)}, bf16[8,1,128,320]{2,3,1,0:T(8,128)(2,1)S(1)}, u32[]{:S(2)}, u32[]{:S(2)}) collective-permute-start(bf16[8,1,128,320]{2,3,1,0:T(8,128)(2,1)S(1)} %get-tuple-element.7), channel_id=1, source_target_pairs={{1,0},{2,1},{3,2},{4,3},{5,4},{6,5},{7,6},{8,7},{9,8},{10,9},{11,1... | collective-permute-start | bytes 1966088 | tf_op jit(solution)/shard_map/ppermute | solution.py:301
  3.3 4.5 %collective-permute-start = (bf16[8,1,128,320]{2,3,1,0:T(8,128)(2,1)S(1)}, bf16[8,1,128,320]{2,3,1,0:T(8,128)(2,1)S(1)}, u32[]{:S(2)}, u32[]{:S(2)}) collective-permute-start(bf16[8,1,128,320]{2,3,1,0:T(8,128)(2,1)S(1)} %get-tuple-element.8), channel_id=1, source_target_pairs={{0,1},{1,2},{2,3},{3,4},{4,5},{5,6},{6,7},{7,8},{8,9},{9,10},{10,1... | collective-permute-start | bytes 1966088 | tf_op jit(solution)/shard_map/ppermute | solution.py:300
  7.8 0.0 copy-start
  7.9 8.2 %copy.10.x_ref = bf16[8,8,128,320]{3,2,1,0:T(8,128)(2,1)} copy(bf16[8,8,128,320]{2,3,1,0:T(8,128)(2,1)} %param.5) | data formatting | bytes 10485760 | tf_op args[0]
  16.0 0.0 copy-done
  16.0 0.1 broadcast_in_dim.10
  16.1 0.1 broadcast_in_dim.11
  16.2 0.7 broadcast_in_dim.12.mask_ref
  16.9 54.7 %shard_map.55 = bf16[18,4,80,320]{3,2,1,0:T(8,128)(2,1)} custom-call(f32[18,1,320]{2,1,0:T(1,128)} %broadcast_in_dim.12.mask_ref, bf16[18,4,80,320]{3,2,1,0:T(8,128)(2,1)} %bitcast.8, f32[18,4,80,320]{3,2,1,0:T(8,128)} %bitcast.5, bf16[18,4,80,320]{3,2,1,0:T(8,128)(2,1)} %bitcast.9), custom_call_target="tpu_custom_call" | custom-call | tf_op jit(solution)/shard_map/pallas_call | solution.py:218
  71.6 4.8 %fusion.2 = (bf16[9,4,80,320]{3,2,1,0:T(8,128)(2,1)}, bf16[9,4,80,320]{3,2,1,0:T(8,128)(2,1)}) fusion(bf16[18,4,80,320]{3,2,1,0:T(8,128)(2,1)} %shard_map.55), kind=kLoop, calls=%fused_computation.3 | loop fusion | bytes 7372800 | tf_op jit(solution)/shard_map/slice | solution.py:325
  76.4 0.0 collective-permute-done.1
  76.4 1.2 copy.12.bottom_ref
  77.6 0.0 collective-permute-done
  77.6 1.2 copy.11.top_ref
  78.8 26.0 %shard_map.56.x_ref = bf16[8,8,128,320]{3,2,1,0:T(8,128)(2,1)} custom-call(bf16[8,8,128,320]{3,2,1,0:T(8,128)(2,1)} %copy.10.x_ref, bf16[8,1,128,320]{3,2,1,0:T(8,128)(2,1)} %copy.11.top_ref, bf16[8,1,128,320]{3,2,1,0:T(8,128)(2,1)} %copy.12.bottom_ref, bf16[3,3,320,320]{3,2,1,0:T(8,128)(2,1)} %bitcast.7), custom_call_target="tpu_custom_call" | custom-call | tf_op jit(solution)/shard_map/pallas_call | solution.py:307
  104.8 1.6 fusion
  106.4 0.4 copy.13
  106.8 2.7 %collective-permute-start.2 = (bf16[8,1,128,320]{2,3,1,0:T(8,128)(2,1)S(1)}, bf16[8,1,128,320]{2,3,1,0:T(8,128)(2,1)S(1)}, u32[]{:S(2)}, u32[]{:S(2)}) collective-permute-start(bf16[8,1,128,320]{2,3,1,0:T(8,128)(2,1)S(1)} %copy.13), channel_id=1, source_target_pairs={{0,1},{1,2},{2,3},{3,4},{4,5},{5,6},{6,7},{7,8},{8,9},{9,10},{10,1... | collective-permute-start | bytes 1966088 | tf_op jit(solution)/shard_map/ppermute | solution.py:300
  109.4 0.4 copy.14
  109.8 1.9 %collective-permute-start.3 = (bf16[8,1,128,320]{2,3,1,0:T(8,128)(2,1)S(1)}, bf16[8,1,128,320]{2,3,1,0:T(8,128)(2,1)S(1)}, u32[]{:S(2)}, u32[]{:S(2)}) collective-permute-start(bf16[8,1,128,320]{2,3,1,0:T(8,128)(2,1)S(1)} %copy.14), channel_id=1, source_target_pairs={{1,0},{2,1},{3,2},{4,3},{5,4},{6,5},{7,6},{8,7},{9,8},{10,9},{11,1... | collective-permute-start | bytes 1966088 | tf_op jit(solution)/shard_map/ppermute | solution.py:301
  111.7 12.2 %collective-permute-done.2 = bf16[8,1,128,320]{2,3,1,0:T(8,128)(2,1)S(1)} collective-permute-done((bf16[8,1,128,320]{2,3,1,0:T(8,128)(2,1)S(1)}, bf16[8,1,128,320]{2,3,1,0:T(8,128)(2,1)S(1)}, u32[]{:S(2)}, u32[]{:S(2)}) %collective-permute-start.2) | collective-permute-done | bytes 655392 | tf_op jit(solution)/shard_map/ppermute | solution.py:300
  124.0 1.2 copy.15.top_ref
  125.2 0.0 collective-permute-done.3
  125.2 1.2 copy.16.bottom_ref
  126.3 26.0 %shard_map.57 = bf16[8,8,128,320]{3,2,1,0:T(8,128)(2,1)} custom-call(bf16[8,8,128,320]{3,2,1,0:T(8,128)(2,1)} %shard_map.56.x_ref, bf16[8,1,128,320]{3,2,1,0:T(8,128)(2,1)} %copy.15.top_ref, bf16[8,1,128,320]{3,2,1,0:T(8,128)(2,1)} %copy.16.bottom_ref, bf16[3,3,320,320]{3,2,1,0:T(8,128)(2,1)} %bitcast.6), custom_call_target="tpu_custom_call" | custom-call | tf_op jit(solution)/shard_map/pallas_call | solution.py:307
  152.4 8.2 %copy.17 = bf16[8,8,128,320]{2,3,1,0:T(8,128)(2,1)} copy(bf16[8,8,128,320]{3,2,1,0:T(8,128)(2,1)} %shard_map.57) | data formatting | bytes 10485760 | tf_op jit(solution)/shard_map/pallas_call | solution.py:307
  (1 shorter events, 0.0 us)
Async XLA Ops:
  1.4 75.0 %collective-permute-start.1 = (bf16[8,1,128,320]{2,3,1,0:T(8,128)(2,1)S(1)}, bf16[8,1,128,320]{2,3,1,0:T(8,128)(2,1)S(1)}, u32[]{:S(2)}, u32[]{:S(2)}) collective-permute-start(bf16[8,1,128,320]{2,3,1,0:T(8,128)(2,1)S(1)} %get-tuple-element.7), channel_id=1, source_target_pairs={{1,0},{2,1},{3,2},{4,3},{5,4},{6,5},{7,6},{8,7},{9,8},{10,9},{11,1... | collective-permute-start | bytes 1966088 | tf_op jit(solution)/shard_map/ppermute | solution.py:301
  3.3 74.3 %collective-permute-start = (bf16[8,1,128,320]{2,3,1,0:T(8,128)(2,1)S(1)}, bf16[8,1,128,320]{2,3,1,0:T(8,128)(2,1)S(1)}, u32[]{:S(2)}, u32[]{:S(2)}) collective-permute-start(bf16[8,1,128,320]{2,3,1,0:T(8,128)(2,1)S(1)} %get-tuple-element.8), channel_id=1, source_target_pairs={{0,1},{1,2},{2,3},{3,4},{4,5},{5,6},{6,7},{7,8},{8,9},{9,10},{10,1... | collective-permute-start | bytes 1966088 | tf_op jit(solution)/shard_map/ppermute | solution.py:300
  7.8 8.2 %copy-start = (s32[2]{0:T(128)S(1)}, s32[2]{0:T(128)}, u32[]{:S(2)}) copy-start(s32[2]{0:T(128)} %param.9) | copy-start | bytes 28
  106.8 17.2 %collective-permute-start.2 = (bf16[8,1,128,320]{2,3,1,0:T(8,128)(2,1)S(1)}, bf16[8,1,128,320]{2,3,1,0:T(8,128)(2,1)S(1)}, u32[]{:S(2)}, u32[]{:S(2)}) collective-permute-start(bf16[8,1,128,320]{2,3,1,0:T(8,128)(2,1)S(1)} %copy.13), channel_id=1, source_target_pairs={{0,1},{1,2},{2,3},{3,4},{4,5},{5,6},{6,7},{7,8},{8,9},{9,10},{10,1... | collective-permute-start | bytes 1966088 | tf_op jit(solution)/shard_map/ppermute | solution.py:300
  109.8 15.4 %collective-permute-start.3 = (bf16[8,1,128,320]{2,3,1,0:T(8,128)(2,1)S(1)}, bf16[8,1,128,320]{2,3,1,0:T(8,128)(2,1)S(1)}, u32[]{:S(2)}, u32[]{:S(2)}) collective-permute-start(bf16[8,1,128,320]{2,3,1,0:T(8,128)(2,1)S(1)} %copy.14), channel_id=1, source_target_pairs={{1,0},{2,1},{3,2},{4,3},{5,4},{6,5},{7,6},{8,7},{9,8},{10,9},{11,1... | collective-permute-start | bytes 1966088 | tf_op jit(solution)/shard_map/ppermute | solution.py:301

commit v2 on v1

--- a/solution.py
+++ b/solution.py
@@ -227,102 +227,83 @@
             collective_id=0, has_side_effects=True, vmem_limit_bytes=56 << 20
         ),
     )(mask, cut(kernel_weights), cut(kernel_momentum), cut(kernel_grads))
-    return out.reshape(kernels, rows, columns, fan_in, fan_out)
+    return out.reshape(kernels, rows * columns * fan_in, fan_out)
 
 
 def silu(v):
     return v / (1.0 + jnp.exp(-v))
 
 
-def conv_kernel(x_ref, top_ref, bottom_ref, k_ref, o_ref, patch, wide, rest):
-    height, width, channels = x_ref.shape[1:]
-    full = channels // 128 // 2 * 256
-    tail = channels - full
-    reach = 3 * channels
-    span = patch.shape[-1]
+def conv_kernel(x_ref, top_ref, bottom_ref, k_ref, o_ref, patch, wide):
+    height, channels, width = x_ref.shape[1:]
 
     @pl.when(pl.program_id(0) == 0)
     def _():
-        patch[:, :, reach:] = jnp.zeros((height + 2, width, span - reach), jnp.bfloat16)
-        rest[reach:, :] = jnp.zeros((span - reach, rest.shape[1]), jnp.bfloat16)
-        for dr in range(3):
-            base = dr * span
-            wide[base + reach : base + span, :] = jnp.zeros((span - reach, full), jnp.bfloat16)
-            for dc in range(3):
-                low, high = dc * full, 3 * full + dc * tail
-                lanes = slice(dr * tail, (dr + 1) * tail)
-                wide[base + low : base + low + full, :] = k_ref[dr, dc, :full, :full]
-                wide[base + high : base + high + tail, :] = k_ref[dr, dc, full:, :full]
-                rest[low : low + full, lanes] = k_ref[dr, dc, :full, full:]
-                rest[high : high + tail, lanes] = k_ref[dr, dc, full:, full:]
-
-    column = lax.broadcasted_iota(jnp.int32, (width, 1), 0)
-    for row in range(height + 2):
+        wide[...] = k_ref[0].astype(jnp.float32).T.astype(jnp.bfloat16)
+
+    conv_image(x_ref.at[0], top_ref.at[0, 0], bottom_ref.at[0, 0], o_ref.at[0], patch, wide)
+
+
+def conv_image(x_ref, top_ref, bottom_ref, o_ref, patch, wide):
+    height, channels, width = x_ref.shape
+    column = lax.broadcasted_iota(jnp.int32, (1, width), 1)
+
+    def build(row):
         if row == 0:
-            v = top_ref[0, 0]
+            v = top_ref[...]
         elif row == height + 1:
-            v = bottom_ref[0, 0]
+            v = bottom_ref[...]
         else:
-            v = x_ref[0, row - 1]
+            v = x_ref[row - 1]
         a = silu(v.astype(jnp.float32))
-        before = jnp.where(column == 0, 0.0, pltpu.roll(a, 1, 0)).astype(jnp.bfloat16)
-        after = jnp.where(column == width - 1, 0.0, pltpu.roll(a, width - 1, 0)).astype(jnp.bfloat16)
-        for dc, part in enumerate((before, a.astype(jnp.bfloat16), after)):
-            patch[row, :, dc * full : (dc + 1) * full] = part[:, :full]
-            high = 3 * full + dc * tail
-            patch[row, :, high : high + tail] = part[:, full:]
-
-    cells = height * width
-    lhs = jnp.concatenate(
-        [patch[dr : dr + height].reshape(cells, span) for dr in range(3)], axis=-1
-    )
-    main = jnp.dot(lhs, wide[...], preferred_element_type=jnp.float32)
-    side = jnp.dot(
-        patch[...].reshape((height + 2) * width, span), rest[...], preferred_element_type=jnp.float32
-    )
-    side = (
-        side[:cells, :tail]
-        + side[width : width + cells, tail : 2 * tail]
-        + side[2 * width : 2 * width + cells, 2 * tail : 3 * tail]
-    )
-    x = x_ref[0].reshape(cells, channels)
-    o_ref[0, :, :, :full] = (
-        (x[:, :full].astype(jnp.float32) + main).astype(o_ref.dtype).reshape(height, width, full)
-    )
-    o_ref[0, :, :, full:] = (
-        (x[:, full:].astype(jnp.float32) + side).astype(o_ref.dtype).reshape(height, width, tail)
-    )
-
-
-def residual_conv(x, kernel):
-    images, height, width, channels = x.shape
+        before = jnp.where(column == 0, 0.0, pltpu.roll(a, 1, 1))
+        after = jnp.where(column == width - 1, 0.0, pltpu.roll(a, width - 1, 1))
+        for dc, part in enumerate((before, a, after)):
+            patch[row, dc * channels : (dc + 1) * channels] = part.astype(jnp.bfloat16)
+
+    built = 0
+    for row in range(0, height, 2):
+        while built < row + 4:
+            build(built)
+            built += 1
+        rhs = jnp.concatenate(
+            [
+                jnp.concatenate([patch[row + dr], patch[row + dr + 1]], axis=1)
+                for dr in range(3)
+            ],
+            axis=0,
+        )
+        acc = jnp.dot(wide[...], rhs, preferred_element_type=jnp.float32)
+        for i in range(2):
+            x = x_ref[row + i].astype(jnp.float32)
+            o_ref[row + i] = (x + acc[:, i * width : (i + 1) * width]).astype(o_ref.dtype)
+
+
+def residual_conv(x, kernels, which):
+    images, height, channels, width = x.shape
     count = lax.axis_size("dp")
     top = lax.ppermute(x[:, -1:], "dp", [(i, i + 1) for i in range(count - 1)])
     bottom = lax.ppermute(x[:, :1], "dp", [(i + 1, i) for i in range(count - 1)])
-    full = channels // 128 // 2 * 256
-    tail = channels - full
-    span = -(-3 * channels // 256) * 256
-    image = pl.BlockSpec((1, height, width, channels), lambda i: (i, 0, 0, 0))
-    edge = pl.BlockSpec((1, 1, width, channels), lambda i: (i, 0, 0, 0))
+    image = pl.BlockSpec((1, height, channels, width), lambda i: (i, 0, 0, 0))
+    edge = pl.BlockSpec((1, 1, channels, width), lambda i: (i, 0, 0, 0))
     return pl.pallas_call(
         conv_kernel,
         out_shape=jax.ShapeDtypeStruct(x.shape, x.dtype),
         grid=(images,),
-        in_specs=[image, edge, edge, pl.BlockSpec(kernel.shape, lambda i: (0, 0, 0, 0))],
+        in_specs=[image, edge, edge, pl.BlockSpec((1,) + kernels.shape[1:], lambda i: (which, 0, 0))],
         out_specs=image,
         scratch_shapes=[
-            pltpu.VMEM((height + 2, width, span), jnp.bfloat16),
-            pltpu.VMEM((3 * span, full), jnp.bfloat16),
-            pltpu.VMEM((span, 3 * tail), jnp.bfloat16),
+            pltpu.VMEM((height + 2, 3 * channels, width), jnp.bfloat16),
+            pltpu.VMEM(kernels.shape[:0:-1], jnp.bfloat16),
         ],
         compiler_params=pltpu.CompilerParams(vmem_limit_bytes=56 << 20),
-    )(x, top, bottom, kernel)
+    )(x, top, bottom, kernels)
 
 
 def local(images, kernel_weights, kernel_momentum, kernel_grads, owners):
     kernels = spread(kernel_weights, kernel_momentum, kernel_grads, owners)
-    hidden = residual_conv(images, kernels[0])
-    return residual_conv(hidden, kernels[1])
+    hidden = residual_conv(images.transpose(0, 1, 3, 2), kernels, 0)
+    return residual_conv(hidden, kernels, 1).transpose(0, 1, 3, 2)
 
 
 def solution(mesh):

time: 161 us -> 143 us (0.89)
  local copies, waits for them, and re-layouts: 30.5 us -> 5.47 us
  Pallas kernels: 107 us -> 111 us
    pallas_call x1, Pallas kernels: 54.7 us -> 63.8 us  [spread(): pl.pallas_call(functools.partial(spread_kernel, groups, dp // 4, chunks),...]
    pallas_call x1 -> x0, local copies, waits for them, and re-layouts: 8.19 us -> none  [residual_conv(): pl.pallas_call(conv_kernel, out_shape=jax.ShapeDtypeStruct(x.shape, x.dty...]
    ppermute x2, waiting for transfers between devices: 0.01 us -> 6.33 us  [residual_conv(): lax.ppermute(x[:, :1], 'dp', [(i + 1, i) for i in range(count - 1)])]
    unnamed x3 -> x8, local copies, waits for them, and re-layouts: 8.19 us -> 1.87 us
    pallas_call x2, Pallas kernels: 52.1 us -> 46.7 us  [residual_conv(): pl.pallas_call(conv_kernel, out_shape=jax.ShapeDtypeStruct(x.shape, x.dty...]
    slice x2 -> x0, local copies, waits for them, and re-layouts: 5.18 us -> none  [the longest x1 4.83 us: local(): return residual_conv(hidden, kernels[1])]
    ppermute x2, waiting for transfers between devices: 12.2 us -> 7.35 us  [residual_conv(): top = lax.ppermute(x[:, -1:], 'dp', [(i, i + 1) for i in range(count - 1)])]
    ppermute x4 -> x0, local copies, waits for them, and re-layouts: 4.77 us -> none  [the longest x2 2.42 us: residual_conv(): top = lax.ppermute(x[:, -1:], 'dp', [(i, i + 1) for i in range(count - 1)])]
  transfers between devices with their start and end apart: 4 -> 4, of which waited for: 1 -> 2; matrix products, arithmetic and copies ran while one was open for 10% -> 1% of each run, Pallas kernels for 34% -> 45%
where the time goes in v2:
time: 143 us; the launch traced here: 142 us
  Pallas kernels  111 us (78%)
  waiting for transfers between devices  13.7 us (10%)
  starting transfers between devices  12 us (8%)
  local copies, waits for them, and re-layouts  5.47 us (4%)
    pallas_call x1, Pallas kernels, spread(): pl.pallas_call(functools.partial(spread_kernel, groups, dp // 4, chunks),...  63.8 us
    pallas_call x2, Pallas kernels, residual_conv(): pl.pallas_call(conv_kernel, out_shape=jax.ShapeDtypeStruct(x.shape, x.dty...  46.7 us
    ppermute x2, starting transfers between devices, residual_conv(): top = lax.ppermute(x[:, -1:], 'dp', [(i, i + 1) for i in range(count - 1)])  8.01 us
    ppermute x2, waiting for transfers between devices, residual_conv(): top = lax.ppermute(x[:, -1:], 'dp', [(i, i + 1) for i in range(count - 1)])  7.35 us
    ppermute x2, waiting for transfers between devices, residual_conv(): lax.ppermute(x[:, :1], 'dp', [(i + 1, i) for i in range(count - 1)])  6.33 us
    ppermute x2, starting transfers between devices, residual_conv(): lax.ppermute(x[:, :1], 'dp', [(i + 1, i) for i in range(count - 1)])  3.99 us
  transfers between devices with their start and end apart: 4, of which 2 were waited for; matrix products, arithmetic and copies ran while one was open for 1% of the time, Pallas kernels for 45%

profile of v2, /device:TPU:1, one launch (start us, length us, event | category | flops | bytes accessed | tf_op | source)
XLA Modules:
  0.0 142.4 jit_solution(6741968044300421204)
XLA Ops:
  0.0 1.4 fusion.1
  1.4 1.9 %collective-permute-start.1 = (bf16[8,1,320,128]{3,2,1,0:T(8,128)(2,1)S(1)}, bf16[8,1,320,128]{3,2,1,0:T(8,128)(2,1)S(1)}, u32[]{:S(2)}, u32[]{:S(2)}) collective-permute-start(bf16[8,1,320,128]{3,2,1,0:T(8,128)(2,1)S(1)} %get-tuple-element.7), channel_id=1, source_target_pairs={{1,0},{2,1},{3,2},{4,3},{5,4},{6,5},{7,6},{8,7},{9,8},{10,9},{11,1... | collective-permute-start | bytes 1966088 | tf_op jit(solution)/shard_map/ppermute | solution.py:286
  3.3 4.5 %collective-permute-start = (bf16[8,1,320,128]{3,2,1,0:T(8,128)(2,1)S(1)}, bf16[8,1,320,128]{3,2,1,0:T(8,128)(2,1)S(1)}, u32[]{:S(2)}, u32[]{:S(2)}) collective-permute-start(bf16[8,1,320,128]{3,2,1,0:T(8,128)(2,1)S(1)} %get-tuple-element.8), channel_id=1, source_target_pairs={{0,1},{1,2},{2,3},{3,4},{4,5},{5,6},{6,7},{7,8},{8,9},{9,10},{10,1... | collective-permute-start | bytes 1966088 | tf_op jit(solution)/shard_map/ppermute | solution.py:285
  7.8 0.7 compare_convert_fusion
  8.5 0.1 broadcast_in_dim.10
  8.6 0.1 broadcast_in_dim.11
  8.7 0.7 broadcast_in_dim.12.mask_ref
  9.4 63.8 %shard_map.55 = bf16[18,4,80,320]{3,2,1,0:T(8,128)(2,1)} custom-call(f32[18,1,320]{2,1,0:T(1,128)} %broadcast_in_dim.12.mask_ref, bf16[18,4,80,320]{3,2,1,0:T(8,128)(2,1)} %bitcast.11, f32[18,4,80,320]{3,2,1,0:T(8,128)} %bitcast.8, bf16[18,4,80,320]{3,2,1,0:T(8,128)(2,1)} %bitcast.12), custom_call_target="tpu_custom_call" | custom-call | tf_op jit(solution)/shard_map/pallas_call | solution.py:218
  73.2 0.0 collective-permute-done.1.bottom_ref
  73.2 0.0 copy-start
  73.2 0.0 collective-permute-done.top_ref
  73.2 0.0 copy-start.1
  73.2 0.8 copy-done
  74.0 0.2 copy-done.1
  74.2 23.4 %shard_map.56.x_ref = bf16[8,8,320,128]{3,2,1,0:T(8,128)(2,1)} custom-call(bf16[8,8,320,128]{3,2,1,0:T(8,128)(2,1)} %bitcast.10, bf16[8,1,320,128]{3,2,1,0:T(8,128)(2,1)} %copy-done.1, bf16[8,1,320,128]{3,2,1,0:T(8,128)(2,1)} %copy-done, bf16[2,2880,320]{2,1,0:T(8,128)(2,1)} %bitcast.6), custom_call_target="tpu_custom_call" | custom-call | tf_op jit(solution)/shard_map/pallas_call | solution.py:289
  97.6 1.4 fusion
  99.0 2.1 %collective-permute-start.3 = (bf16[8,1,320,128]{3,2,1,0:T(8,128)(2,1)S(1)}, bf16[8,1,320,128]{3,2,1,0:T(8,128)(2,1)S(1)}, u32[]{:S(2)}, u32[]{:S(2)}) collective-permute-start(bf16[8,1,320,128]{3,2,1,0:T(8,128)(2,1)S(1)} %get-tuple-element.5), channel_id=1, source_target_pairs={{1,0},{2,1},{3,2},{4,3},{5,4},{6,5},{7,6},{8,7},{9,8},{10,9},{11,1... | collective-permute-start | bytes 1966088 | tf_op jit(solution)/shard_map/ppermute | solution.py:286
  101.1 3.5 %collective-permute-start.2 = (bf16[8,1,320,128]{3,2,1,0:T(8,128)(2,1)S(1)}, bf16[8,1,320,128]{3,2,1,0:T(8,128)(2,1)S(1)}, u32[]{:S(2)}, u32[]{:S(2)}) collective-permute-start(bf16[8,1,320,128]{3,2,1,0:T(8,128)(2,1)S(1)} %get-tuple-element.6), channel_id=1, source_target_pairs={{0,1},{1,2},{2,3},{3,4},{4,5},{5,6},{6,7},{7,8},{8,9},{9,10},{10,1... | collective-permute-start | bytes 1966088 | tf_op jit(solution)/shard_map/ppermute | solution.py:285
  104.6 6.3 %collective-permute-done.3.bottom_ref = bf16[8,1,320,128]{3,2,1,0:T(8,128)(2,1)S(1)} collective-permute-done((bf16[8,1,320,128]{3,2,1,0:T(8,128)(2,1)S(1)}, bf16[8,1,320,128]{3,2,1,0:T(8,128)(2,1)S(1)}, u32[]{:S(2)}, u32[]{:S(2)}) %collective-permute-start.3) | collective-permute-done | bytes 655392 | tf_op jit(solution)/shard_map/ppermute | solution.py:286
  110.9 0.0 copy-start.2
  110.9 7.3 %collective-permute-done.2.top_ref = bf16[8,1,320,128]{3,2,1,0:T(8,128)(2,1)S(1)} collective-permute-done((bf16[8,1,320,128]{3,2,1,0:T(8,128)(2,1)S(1)}, bf16[8,1,320,128]{3,2,1,0:T(8,128)(2,1)S(1)}, u32[]{:S(2)}, u32[]{:S(2)}) %collective-permute-start.2) | collective-permute-done | bytes 655392 | tf_op jit(solution)/shard_map/ppermute | solution.py:285
  118.2 0.0 copy-done.2
  118.2 0.0 copy-start.3
  118.2 0.8 copy-done.3
  119.1 23.4 %shard_map.57 = bf16[8,8,320,128]{3,2,1,0:T(8,128)(2,1)} custom-call(bf16[8,8,320,128]{3,2,1,0:T(8,128)(2,1)} %shard_map.56.x_ref, bf16[8,1,320,128]{3,2,1,0:T(8,128)(2,1)} %copy-done.3, bf16[8,1,320,128]{3,2,1,0:T(8,128)(2,1)} %copy-done.2, bf16[2,2880,320]{2,1,0:T(8,128)(2,1)} %bitcast.7), custom_call_target="tpu_custom_call" | custom-call | tf_op jit(solution)/shard_map/pallas_call | solution.py:289
Async XLA Ops:
  1.4 71.8 %collective-permute-start.1 = (bf16[8,1,320,128]{3,2,1,0:T(8,128)(2,1)S(1)}, bf16[8,1,320,128]{3,2,1,0:T(8,128)(2,1)S(1)}, u32[]{:S(2)}, u32[]{:S(2)}) collective-permute-start(bf16[8,1,320,128]{3,2,1,0:T(8,128)(2,1)S(1)} %get-tuple-element.7), channel_id=1, source_target_pairs={{1,0},{2,1},{3,2},{4,3},{5,4},{6,5},{7,6},{8,7},{9,8},{10,9},{11,1... | collective-permute-start | bytes 1966088 | tf_op jit(solution)/shard_map/ppermute | solution.py:286
  3.3 69.9 %collective-permute-start = (bf16[8,1,320,128]{3,2,1,0:T(8,128)(2,1)S(1)}, bf16[8,1,320,128]{3,2,1,0:T(8,128)(2,1)S(1)}, u32[]{:S(2)}, u32[]{:S(2)}) collective-permute-start(bf16[8,1,320,128]{3,2,1,0:T(8,128)(2,1)S(1)} %get-tuple-element.8), channel_id=1, source_target_pairs={{0,1},{1,2},{2,3},{3,4},{4,5},{5,6},{6,7},{7,8},{8,9},{9,10},{10,1... | collective-permute-start | bytes 1966088 | tf_op jit(solution)/shard_map/ppermute | solution.py:285
  73.2 0.8 copy-start
  73.2 1.0 copy-start.1
  99.0 11.9 %collective-permute-start.3 = (bf16[8,1,320,128]{3,2,1,0:T(8,128)(2,1)S(1)}, bf16[8,1,320,128]{3,2,1,0:T(8,128)(2,1)S(1)}, u32[]{:S(2)}, u32[]{:S(2)}) collective-permute-start(bf16[8,1,320,128]{3,2,1,0:T(8,128)(2,1)S(1)} %get-tuple-element.5), channel_id=1, source_target_pairs={{1,0},{2,1},{3,2},{4,3},{5,4},{6,5},{7,6},{8,7},{9,8},{10,9},{11,1... | collective-permute-start | bytes 1966088 | tf_op jit(solution)/shard_map/ppermute | solution.py:286
  101.1 17.2 %collective-permute-start.2 = (bf16[8,1,320,128]{3,2,1,0:T(8,128)(2,1)S(1)}, bf16[8,1,320,128]{3,2,1,0:T(8,128)(2,1)S(1)}, u32[]{:S(2)}, u32[]{:S(2)}) collective-permute-start(bf16[8,1,320,128]{3,2,1,0:T(8,128)(2,1)S(1)} %get-tuple-element.6), channel_id=1, source_target_pairs={{0,1},{1,2},{2,3},{3,4},{4,5},{5,6},{6,7},{7,8},{8,9},{9,10},{10,1... | collective-permute-start | bytes 1966088 | tf_op jit(solution)/shard_map/ppermute | solution.py:285
  110.9 7.4 %copy-start.2 = (bf16[8,1,320,128]{3,2,1,0:T(8,128)(2,1)}, bf16[8,1,320,128]{3,2,1,0:T(8,128)(2,1)S(1)}, u32[]{:S(2)}) copy-start(bf16[8,1,320,128]{3,2,1,0:T(8,128)(2,1)S(1)} %collective-permute-done.3.bottom_ref) | copy-start | bytes 1966084
  118.2 0.8 copy-start.3

commit v3 on v0

v3 whole, which is shorter than its diff:
```python
import functools

import jax
import jax.numpy as jnp
from jax import lax
from jax.experimental import pallas as pl
from jax.experimental.pallas import tpu as pltpu
from jax.sharding import PartitionSpec as P

momentum_decay = 0.9
learn_rate = 0.5
MESH = pl.DeviceIdType.MESH
fine_chunks = 15
coarse_chunks = 3
pair_hop = 3
hop = 4


class Place:
    def __init__(self, groups, dp):
        self.groups, self.dp, self.last = groups, dp, dp // 4 - 1
        self.group, self.at = lax.axis_index("groups"), lax.axis_index("dp")
        self.z, self.y, self.core = self.at // 4, (self.at // 2) % 2, self.at % 2
        self.mate = self.at + 1 - 2 * self.core
        self.beside = self.at - 1 + 2 * self.core
        self.across = self.at + 2 - 4 * self.y
        self.share = 2 * self.group + self.core
        self.others = [lax.rem(self.group + step, groups) for step in range(1, groups)]
        self.has_beside = (self.beside >= 0) & (self.beside < dp)

    def meet(self):
        barrier = pltpu.get_barrier_semaphore()

        def greet(**where):
            pl.semaphore_signal(barrier, inc=1, device_id=where, device_id_type=MESH)

        greet(dp=self.mate)
        greet(dp=self.across)
        for other in self.others:
            greet(groups=other)
        pl.when(self.has_beside)(lambda: greet(dp=self.beside))
        pl.when(self.z > 0)(lambda: greet(dp=self.at - 4))
        pl.when(self.z < self.last)(lambda: greet(dp=self.at + 4))
        more = [
            jnp.where(there, 1, 0)
            for there in (self.has_beside, self.z > 0, self.z < self.last)
        ]
        pl.semaphore_wait(barrier, 1 + self.groups + sum(more))


def remote(src, dst, sem, k, **where):
    return pltpu.make_async_remote_copy(
        src, dst, sem.at[0, k], sem.at[1, k], device_id=where, device_id_type=MESH
    )


class Stream:
    def __init__(self, place, col, out, col_in, joined, fwd, fwd_in, back, back_in, done, sems):
        self.__dict__.update(place=place, col=col, out=out, col_in=col_in, joined=joined)
        self.__dict__.update(fwd=fwd, fwd_in=fwd_in, back=back, back_in=back_in, done=done)
        self.col_sem, self.fwd_sem, self.back_sem, self.mate_sem = sems[:4]
        self.cross_sem, self.pass_sem, self.keep_sem = sems[4:]

    def to_col(self, k):
        return remote(self.col.at[k], self.col_in.at[k], self.col_sem, k, dp=self.place.across)

    def to_fwd(self, k, up=4):
        return remote(self.fwd.at[k], self.fwd_in.at[k], self.fwd_sem, k, dp=self.place.at + up)

    def to_back(self, k, down=4):
        return remote(self.back.at[k], self.back_in.at[k], self.back_sem, k, dp=self.place.at - down)

    def keep(self, k):
        return pltpu.make_async_copy(
            self.done.at[k], self.out.at[k, self.place.share], self.keep_sem.at[k]
        )

    def to_mate(self, k):
        return remote(
            self.done.at[k], self.out.at[k, self.place.share], self.mate_sem, k, dp=self.place.mate
        )

    def to_cross(self, k, i):
        return remote(
            self.done.at[k], self.out.at[k, self.place.share], self.cross_sem.at[i], k,
            groups=self.place.others[i],
        )

    def to_pass(self, k, i):
        p = self.place
        slot = 2 * lax.rem(p.group + p.groups - 1 - i, p.groups) + p.core
        return remote(self.out.at[k, slot], self.out.at[k, slot], self.pass_sem.at[i], k, dp=p.mate)

    def join_col(self, k):
        self.to_col(k).wait_recv()
        self.joined[k] = self.col[k] + self.col_in[k]

    def go_fwd(self, k):
        p = self.place

        @pl.when(p.z == 0)
        def _():
            self.fwd[k] = self.joined[k]

        @pl.when(p.z > 0)
        def _():
            self.to_fwd(k, -4).wait_recv()
            self.fwd[k] = self.joined[k] + self.fwd_in[k]

        pl.when(p.z < p.last)(lambda: self.to_fwd(k).start())

    def go_back(self, k):
        p = self.place

        @pl.when(p.z == p.last)
        def _():
            self.back[k] = self.joined[k]

        @pl.when(p.z < p.last)
        def _():
            self.to_back(k, -4).wait_recv()
            self.back[k] = self.joined[k] + self.back_in[k]

        pl.when(p.z > 0)(lambda: self.to_back(k).start())

    def finish(self, k):
        p = self.place

        @pl.when(p.z < p.last)
        def _():
            self.done[k] = self.fwd[k] + self.back_in[k]

        @pl.when(p.z == p.last)
        def _():
            self.done[k] = self.fwd[k]

        for i in range(p.groups - 1):
            self.to_cross(k, i).start()
        self.to_mate(k).start()
        self.keep(k).start()

    def pass_on(self, k):
        for i in range(self.place.groups - 1):
            self.to_cross(k, i).wait_recv()
            self.to_pass(k, i).start()

    def steps(self, chunks, hop):
        return chunks + hop * (self.place.last + 2)

    def step(self, t, chunks, hop):
        p = self.place
        at_step(t - hop, chunks, self.join_col)
        at_step(t - hop - p.z * hop, chunks, self.go_fwd)
        at_step(t - hop - (p.last - p.z) * hop, chunks, self.go_back)
        at_step(t - hop - p.last * hop, chunks, self.finish)
        at_step(t - hop - p.last * hop - hop, chunks, self.pass_on)

    def drain(self, k):
        p = self.place
        self.to_col(k).wait_send()
        pl.when(p.z < p.last)(lambda: self.to_fwd(k).wait_send())
        pl.when(p.z > 0)(lambda: self.to_back(k).wait_send())
        self.to_mate(k).wait()
        self.keep(k).wait()
        for i in range(p.groups - 1):
            self.to_cross(k, i).wait_send()
            self.to_pass(k, i).wait()

    @staticmethod
    def scratch(chunks, part, width, groups):
        piece = pltpu.VMEM((chunks, part, width), jnp.bfloat16)
        sems = pltpu.SemaphoreType.DMA((2, chunks))
        many = pltpu.SemaphoreType.DMA((groups - 1, 2, chunks))
        return [piece] * 7 + [sems] * 4 + [many] * 2 + [pltpu.SemaphoreType.DMA((chunks,))]


def at_step(k, chunks, what):
    pl.when((k >= 0) & (k < chunks))(lambda: what(k))


def each(chunks, what):
    def body(k, carry):
        what(k)
        return carry

    lax.fori_loop(0, chunks, body, 0)


class Edges:
    def __init__(self, place, first, final, out, sem):
        self.place, self.first, self.final, self.out, self.sem = place, first, final, out, sem

    def down(self, k, to=1):
        return remote(self.final(k), self.out(0, k), self.sem.at[0], k, dp=self.place.at + to)

    def up(self, k, to=1):
        return remote(self.first(k), self.out(1, k), self.sem.at[1], k, dp=self.place.at - to)

    def start(self, k):
        at, dp = self.place.at, self.place.dp
        pl.when(at < dp - 1)(lambda: self.down(k).start())
        pl.when(at > 0)(lambda: self.up(k).start())

    def drain(self, k):
        at, dp = self.place.at, self.place.dp

        @pl.when(at < dp - 1)
        def _():
            self.down(k).wait_send()
            self.up(k, -1).wait_recv()

        @pl.when(at > 0)
        def _():
            self.up(k).wait_send()
            self.down(k, -1).wait_recv()


class Renewal:
    def __init__(self, place, mask, base, state, bufs, col, pair_out, pair_in, load_sem, pair_sem):
        self.place, self.mask, self.base = place, mask, base
        self.state, self.bufs = state, bufs
        self.col, self.pair_out, self.pair_in = col, pair_out, pair_in
        self.load_sem, self.pair_sem = load_sem, pair_sem

    def loads(self, k):
        src = pl.ds(2 * self.place.group, 2)
        return [
            pltpu.make_async_copy(ref.at[self.base + k, src], buf.at[k], self.load_sem.at[i, k])
            for i, (ref, buf) in enumerate(zip(self.state, self.bufs))
        ]

    def start(self, k):
        for copy in self.loads(k):
            copy.start()

    def to_pair(self, k):
        return remote(
            self.pair_out.at[k], self.pair_in.at[k], self.pair_sem, k, dp=self.place.mate
        )

    def renew(self, k):
        for copy in self.loads(k):
            copy.wait()
        w, m, g = self.bufs
        mine = self.mask > 0.5

        def new(c):
            velocity = momentum_decay * m[k, c] + g[k, c].astype(jnp.float32)
            updated = w[k, c].astype(jnp.float32) - learn_rate * velocity
            return jnp.where(mine, updated, 0.0).astype(jnp.bfloat16)

        self.pair_out[k] = new(1 - self.place.core)
        self.to_pair(k).start()
        self.col[k] = new(self.place.core)

    def join(self, k):
        self.to_pair(k).wait_recv()
        self.col[k] = self.col[k] + self.pair_in[k]

    @staticmethod
    def scratch(chunks, part, width):
        load = lambda dtype: pltpu.VMEM((chunks, 2, part, width), dtype)
        piece = pltpu.VMEM((chunks, part, width), jnp.bfloat16)
        return [load(jnp.bfloat16), load(jnp.float32), load(jnp.bfloat16), piece, piece] + [
            pltpu.SemaphoreType.DMA((3, chunks)),
            pltpu.SemaphoreType.DMA((2, chunks)),
        ]


def spread_kernel(groups, dp, mask_ref, *refs):
    first_state, second_state, x_ref, out_ref, col1_ref, rims_ref = (
        refs[:3], refs[3:6], refs[6], refs[7], refs[8], refs[9],
    )
    scratch = refs[10:]
    place = Place(groups, dp)
    one = Renewal(place, mask_ref[0], 0, first_state, scratch[:3], scratch[14], *scratch[3:7])
    two = Renewal(place, mask_ref[1], coarse_chunks, second_state, scratch[7:10], col1_ref, *scratch[10:14])
    stream = Stream(place, scratch[14], out_ref, *scratch[15:22], scratch[22:29])
    height = x_ref.shape[1]
    edges = Edges(
        place, lambda k: x_ref.at[:, 0], lambda k: x_ref.at[:, height - 1],
        lambda side, k: rims_ref.at[side], scratch[29],
    )
    each(fine_chunks, one.start)
    each(coarse_chunks, two.start)
    place.meet()

    def join(k):
        one.join(k)
        stream.to_col(k).start()

    def step(t, carry):
        at_step(t, fine_chunks, one.renew)
        at_step(t - pair_hop, fine_chunks, join)
        stream.step(t - pair_hop, fine_chunks, hop)
        late = t - fine_chunks - pair_hop
        pl.when(late == 0)(lambda: edges.start(0))
        at_step(late - 1, coarse_chunks, two.renew)
        at_step(late - 1 - pair_hop, coarse_chunks, two.join)
        return carry

    lax.fori_loop(0, pair_hop + stream.steps(fine_chunks, hop), step, 0)

    def drain(k):
        one.to_pair(k).wait_send()
        stream.drain(k)

    each(fine_chunks, drain)
    each(coarse_chunks, lambda k: two.to_pair(k).wait_send())
    edges.drain(0)


def spread(kernel_weights, kernel_momentum, kernel_grads, owners, x):
    groups, dp = lax.axis_size("groups"), lax.axis_size("dp")
    _, _, rows, columns, fan_in, fan_out = kernel_weights.shape
    images, _, channels, width = x.shape
    shares, depth = 2 * groups, rows * columns * fan_in
    mine = (owners == lax.axis_index("dp")).astype(jnp.float32)
    mask = jnp.broadcast_to(mine[:, None, None], (2, 1, fan_out))
    state = (kernel_weights, kernel_momentum, kernel_grads)

    def cut(chunks):
        return [a.reshape(2 * chunks, shares, -1, fan_out) for a in state]

    fine, coarse = depth // fine_chunks // shares, depth // coarse_chunks // shares
    any_space = pl.BlockSpec(memory_space=pl.ANY)
    vmem = pl.BlockSpec(memory_space=pltpu.VMEM)
    kernel, col, rims = pl.pallas_call(
        functools.partial(spread_kernel, groups, dp),
        out_shape=[
            jax.ShapeDtypeStruct((fine_chunks, shares, fine, fan_out), jnp.bfloat16),
            jax.ShapeDtypeStruct((coarse_chunks, coarse, fan_out), jnp.bfloat16),
            jax.ShapeDtypeStruct((2, images, channels, width), jnp.bfloat16),
        ],
        in_specs=[vmem] + [any_space] * 7,
        out_specs=[vmem, vmem, any_space],
        scratch_shapes=Renewal.scratch(fine_chunks, fine, fan_out)
        + Renewal.scratch(coarse_chunks, coarse, fan_out)
        + [pltpu.VMEM((fine_chunks, fine, fan_out), jnp.bfloat16)]
        + Stream.scratch(fine_chunks, fine, fan_out, groups)
        + [pltpu.SemaphoreType.DMA((2, 2, 1))],
        compiler_params=pltpu.CompilerParams(
            collective_id=0, has_side_effects=True, vmem_limit_bytes=56 << 20
        ),
    )(mask, *cut(fine_chunks), *cut(coarse_chunks), x)
    return kernel.reshape(depth, fan_out), col, rims


def silu(v):
    return v / (1.0 + jnp.exp(-v))


def conv_image(x_ref, top_ref, bottom_ref, o_ref, patch, wide):
    height, channels, width = x_ref.shape
    at = lax.axis_index("dp")
    column = lax.broadcasted_iota(jnp.int32, (1, width), 1)

    def build(row):
        if row == 0:
            v = jnp.where(at > 0, top_ref[...].astype(jnp.float32), 0.0)
        elif row == height + 1:
            v = jnp.where(at < lax.axis_size("dp") - 1, bottom_ref[...].astype(jnp.float32), 0.0)
        else:
            v = x_ref[row - 1]
        a = silu(v.astype(jnp.float32))
        before = jnp.where(column == 0, 0.0, pltpu.roll(a, 1, 1))
        after = jnp.where(column == width - 1, 0.0, pltpu.roll(a, width - 1, 1))
        for dc, part in enumerate((before, a, after)):
            patch[row, dc * channels : (dc + 1) * channels] = part.astype(jnp.bfloat16)

    built = 0
    for row in range(0, height, 2):
        while built < row + 4:
            build(built)
            built += 1
        rhs = jnp.concatenate(
            [
                jnp.concatenate([patch[row + dr], patch[row + dr + 1]], axis=1)
                for dr in range(3)
            ],
            axis=0,
        )
        acc = jnp.dot(wide[...], rhs, preferred_element_type=jnp.float32)
        for i in range(2):
            x = x_ref[row + i].astype(jnp.float32)
            o_ref[row + i] = (x + acc[:, i * width : (i + 1) * width]).astype(o_ref.dtype)


def first_kernel(groups, dp, x_ref, top_ref, bottom_ref, k_ref, col_ref, o_ref, out_ref, rims_ref,
                 patch, wide, borders, edge_sem, *scratch):
    place = Place(groups, dp)
    image, images = pl.program_id(0), pl.num_programs(0)
    height = x_ref.shape[1]
    stream = Stream(place, col_ref, out_ref, *scratch[:7], scratch[7:])
    edges = Edges(
        place, lambda k: borders.at[k, 0], lambda k: borders.at[k, 1],
        lambda side, k: rims_ref.at[side, k], edge_sem,
    )

    @pl.when(image == 0)
    def _():
        place.meet()
        wide[...] = k_ref[...].astype(jnp.float32).T.astype(jnp.bfloat16)

    def step(t, carry=0):
        at_step(t, coarse_chunks, lambda k: stream.to_col(k).start())
        stream.step(t, coarse_chunks, 1)
        return carry

    step(image)
    conv_image(x_ref.at[0], top_ref.at[0, 0], bottom_ref.at[0, 0], o_ref.at[0], patch, wide)
    borders[image, 0] = o_ref[0, 0]
    borders[image, 1] = o_ref[0, height - 1]
    edges.start(image)

    @pl.when(image == images - 1)
    def _():
        count = borders.shape[0]
        lax.fori_loop(count, max(count, stream.steps(coarse_chunks, 1)), step, 0)
        each(coarse_chunks, stream.drain)
        each(count, edges.drain)


def second_kernel(x_ref, top_ref, bottom_ref, k_ref, o_ref, patch, wide):
    @pl.when(pl.program_id(0) == 0)
    def _():
        wide[...] = k_ref[...].astype(jnp.float32).T.astype(jnp.bfloat16)

    conv_image(x_ref.at[0], top_ref.at[0, 0], bottom_ref.at[0, 0], o_ref.at[0], patch, wide)


def conv_specs(x, kernel):
    images, height, channels, width = x.shape
    image = pl.BlockSpec((1, height, channels, width), lambda i: (i, 0, 0, 0))
    top = pl.BlockSpec((1, 1, channels, width), lambda i: (0, i, 0, 0))
    bottom = pl.BlockSpec((1, 1, channels, width), lambda i: (1, i, 0, 0))
    scratch = [
        pltpu.VMEM((height + 2, 3 * channels, width), jnp.bfloat16),
        pltpu.VMEM(kernel.shape[::-1], jnp.bfloat16),
    ]
    return image, [image, top, bottom, pl.BlockSpec(kernel.shape, lambda i: (0, 0))], scratch


def first_conv(x, rims, kernel, col):
    groups, dp = lax.axis_size("groups"), lax.axis_size("dp")
    images, height, channels, width = x.shape
    chunks, part, fan_out = col.shape
    image, in_specs, scratch = conv_specs(x, kernel)
    any_space = pl.BlockSpec(memory_space=pl.ANY)
    hidden, second, rims = pl.pallas_call(
        functools.partial(first_kernel, groups, dp),
        out_shape=[
            jax.ShapeDtypeStruct(x.shape, x.dtype),
            jax.ShapeDtypeStruct((chunks, 2 * groups, part, fan_out), jnp.bfloat16),
            jax.ShapeDtypeStruct(rims.shape, rims.dtype),
        ],
        grid=(images,),
        in_specs=in_specs + [pl.BlockSpec(col.shape, lambda i: (0, 0, 0))],
        out_specs=[image, any_space, any_space],
        scratch_shapes=scratch
        + [
            pltpu.VMEM((images, 2, channels, width), jnp.bfloat16),
            pltpu.SemaphoreType.DMA((2, 2, images)),
        ]
        + Stream.scratch(chunks, part, fan_out, groups),
        compiler_params=pltpu.CompilerParams(
            collective_id=1, has_side_effects=True, vmem_limit_bytes=56 << 20
        ),
    )(x, rims, rims, kernel, col)
    return hidden, second.reshape(kernel.shape), rims


def second_conv(x, rims, kernel):
    image, in_specs, scratch = conv_specs(x, kernel)
    return pl.pallas_call(
        second_kernel,
        out_shape=jax.ShapeDtypeStruct(x.shape, x.dtype),
        grid=(x.shape[0],),
        in_specs=in_specs,
        out_specs=image,
        scratch_shapes=scratch,
        compiler_params=pltpu.CompilerParams(vmem_limit_bytes=56 << 20),
    )(x, rims, rims, kernel)


def local(images, kernel_weights, kernel_momentum, kernel_grads, owners):
    x = images.transpose(0, 1, 3, 2)
    kernel, col, rims = spread(kernel_weights, kernel_momentum, kernel_grads, owners, x)
    hidden, kernel, rims = first_conv(x, rims, kernel, col)
    return second_conv(hidden, rims, kernel).transpose(0, 1, 3, 2)


def solution(mesh):
    placed = (
        P("groups", "dp", None, None),
        P("dp", None, None, None, None, None),
        P("dp", None, None, None, None, None),
        P("dp", None, None, None, None, None),
        P(),
    )
    return jax.shard_map(
        local, mesh=mesh, in_specs=placed, out_specs=P("groups", "dp", None, None), check_vma=False
    )
```

time: 240 us -> 122 us (0.51)
  Pallas kernels: 0 us -> 120 us
  waiting for transfers between devices: 105 us -> 0 us
  matrix products: 62.2 us -> 0 us
  local copies, waits for them, and re-layouts: 28.2 us -> 0.65 us
  between operations: 14.7 us -> 0.02 us
  other arithmetic: 14.8 us -> 0.66 us
  starting transfers between devices: 13.9 us -> 0 us
    pallas_call x0 -> x3, Pallas kernels: none -> 120 us  [the longest x1 49.9 us: first_conv(): pl.pallas_call(functools.partial(first_kernel, groups, dp), out_shape=[ja...]
    psum x1 -> x0, waiting for transfers between devices: 83.4 us -> none  [from_root(): return lax.psum(jnp.where(mine, x, jnp.zeros_like(x)), axis)]
    conv_general_dilated x2 -> x0, matrix products: 62.2 us -> none  [conv_rows(): lax.conv_general_dilated(activated, kernel, (1, 1), ((0, 0), (1, 1)), dim...]
    ppermute x4 -> x0, waiting for transfers between devices: 21.8 us -> none  [the longest x2 13.8 us: padded(): lax.ppermute(head, axis, [((i + 1) % count, i) for i in range(ends)])]
    ppermute x4 -> x0, starting transfers between devices: 13.9 us -> none  [the longest x2 7.59 us: padded(): lax.ppermute(tail, axis, [(i, (i + 1) % count) for i in range(ends)])]
    unnamed x5 -> x0, local copies, waits for them, and re-layouts: 13.8 us -> none
    select_n x1 -> x0, other arithmetic: 9.39 us -> none  [from_root(): return lax.psum(jnp.where(mine, x, jnp.zeros_like(x)), axis)]
    convert_element_type x1 -> x0, local copies, waits for them, and re-layouts: 8.51 us -> none  [local(): return residual_conv(hidden, second_kernel).astype(jnp.bfloat16)]
  transfers between devices with their start and end apart: 5 -> 0, of which waited for: 5 -> 0; matrix products, arithmetic and copies ran while one was open for 7% -> 0% of each run, Pallas kernels for 0% -> 0%
where the time goes in v3:
time: 122 us
  Pallas kernels  120 us (98%)
    pallas_call x1, Pallas kernels, first_conv(): pl.pallas_call(functools.partial(first_kernel, groups, dp), out_shape=[ja...  49.9 us
    pallas_call x1, Pallas kernels, spread(): pl.pallas_call(functools.partial(spread_kernel, groups, dp), out_shape=[j...  47 us
    pallas_call x1, Pallas kernels, second_conv(): pl.pallas_call(second_kernel, out_shape=jax.ShapeDtypeStruct(x.shape, x.d...  23.4 us

profile of v3, /device:TPU:1, one launch (start us, length us, event | category | flops | bytes accessed | tf_op | source)
XLA Modules:
  0.0 121.7 jit_solution(6233387128461608392)
XLA Ops:
  0.0 0.7 compare_convert_fusion
  0.7 0.7 broadcast_in_dim.2.mask_ref
  1.3 47.0 %shard_map.55 = (bf16[15,4,48,320]{3,2,1,0:T(8,128)(2,1)}, bf16[3,240,320]{2,1,0:T(8,128)(2,1)}, bf16[2,8,320,128]{3,2,1,0:T(8,128)(2,1)}) custom-call(f32[2,1,320]{2,1,0:T(1,128)} %broadcast_in_dim.2.mask_ref, bf16[30,4,48,320]{3,2,1,0:T(8,128)(2,1)} %bitcast.14, f32[30,4,48,320]{3,2,1,0:T(8,128)} %bitcast.10, bf16[30,4,48,320]{3,2,1,0:T(8,128)(2,1)} %bitcast.16, ...), custom_call_target="tpu_custom_call" | custom-call | tf_op jit(solution)/shard_map/pallas_call | solution.py:328
  48.3 49.9 %shard_map.56 = (bf16[8,8,320,128]{3,2,1,0:T(8,128)(2,1)}, bf16[3,4,240,320]{3,2,1,0:T(8,128)(2,1)}, bf16[2,8,320,128]{3,2,1,0:T(8,128)(2,1)}) custom-call(bf16[8,8,320,128]{3,2,1,0:T(8,128)(2,1)} %bitcast.13, bf16[2,8,320,128]{3,2,1,0:T(8,128)(2,1)} %get-tuple-element.11.top_ref.bottom_ref, bf16[2,8,320,128]{3,2,1,0:T(8,128)(2,1)} %get-tuple-element.11.top_ref.bottom_ref, ...), custom_call_target="tpu_custom_call" | custom-call | tf_op jit(solution)/shard_map/pallas_call | solution.py:450
  98.3 23.4 %shard_map.57 = bf16[8,8,320,128]{3,2,1,0:T(8,128)(2,1)} custom-call(bf16[8,8,320,128]{3,2,1,0:T(8,128)(2,1)} %get-tuple-element.14.x_ref, bf16[2,8,320,128]{3,2,1,0:T(8,128)(2,1)} %get-tuple-element.15.top_ref.bottom_ref, bf16[2,8,320,128]{3,2,1,0:T(8,128)(2,1)} %get-tuple-element.15.top_ref.bottom_ref, bf16[2880,320]{1,0:T(8,128)(2,1)} %bitcast.19), custom_call_target="tpu_custom_call" | custom-call | tf_op jit(solution)/shard_map/pallas_call | solution.py:475

commit v4 on v3

--- a/solution.py
+++ b/solution.py
@@ -174,6 +174,44 @@
         return [piece] * 7 + [sems] * 4 + [many] * 2 + [pltpu.SemaphoreType.DMA((chunks,))]
 
 
+def half_rows(part):
+    return -(-(part // 2) // 8) * 8
+
+
+def packed_rows(part, width):
+    return width // 128 * part + (half_rows(part) if width % 128 else 0)
+
+
+def packed(v):
+    part, width = v.shape
+    full, half = width // 128 * 128, half_rows(part)
+    blocks = [v[:, i : i + 128] for i in range(0, full, 128)]
+    if full < width:
+        low, high = v[:half, full:], v[half:, full:]
+        if part < 2 * half:
+            high = jnp.concatenate(
+                [high, jnp.zeros((2 * half - part, width - full), v.dtype)], axis=0
+            )
+        blocks.append(jnp.concatenate([low, high], axis=1))
+    return jnp.concatenate(blocks, axis=0)
+
+
+def unpack(k_ref, natural):
+    chunks, shares, _, _ = k_ref.shape
+    depth, width = natural.shape
+    part = depth // (chunks * shares)
+    full, half = width // 128 * 128, half_rows(part)
+    for piece in range(chunks * shares):
+        v = k_ref[piece // shares, piece % shares].astype(jnp.float32)
+        base = piece * part
+        for i in range(full // 128):
+            natural[base : base + part, i * 128 : (i + 1) * 128] = v[i * part : (i + 1) * part]
+        if full < width:
+            rest = v[full // 128 * part :]
+            natural[base : base + half, full:] = rest[:, : width - full]
+            natural[base + half : base + part, full:] = rest[: part - half, width - full :]
+
+
 def at_step(k, chunks, what):
     pl.when((k >= 0) & (k < chunks))(lambda: what(k))
 
@@ -247,7 +285,7 @@
         def new(c):
             velocity = momentum_decay * m[k, c] + g[k, c].astype(jnp.float32)
             updated = w[k, c].astype(jnp.float32) - learn_rate * velocity
-            return jnp.where(mine, updated, 0.0).astype(jnp.bfloat16)
+            return packed(jnp.where(mine, updated, 0.0)).astype(jnp.bfloat16)
 
         self.pair_out[k] = new(1 - self.place.core)
         self.to_pair(k).start()
@@ -260,7 +298,7 @@
     @staticmethod
     def scratch(chunks, part, width):
         load = lambda dtype: pltpu.VMEM((chunks, 2, part, width), dtype)
-        piece = pltpu.VMEM((chunks, part, width), jnp.bfloat16)
+        piece = pltpu.VMEM((chunks, packed_rows(part, width), 128), jnp.bfloat16)
         return [load(jnp.bfloat16), load(jnp.float32), load(jnp.bfloat16), piece, piece] + [
             pltpu.SemaphoreType.DMA((3, chunks)),
             pltpu.SemaphoreType.DMA((2, chunks)),
@@ -323,27 +361,28 @@
         return [a.reshape(2 * chunks, shares, -1, fan_out) for a in state]
 
     fine, coarse = depth // fine_chunks // shares, depth // coarse_chunks // shares
+    fine_rows, coarse_rows = packed_rows(fine, fan_out), packed_rows(coarse, fan_out)
     any_space = pl.BlockSpec(memory_space=pl.ANY)
     vmem = pl.BlockSpec(memory_space=pltpu.VMEM)
     kernel, col, rims = pl.pallas_call(
         functools.partial(spread_kernel, groups, dp),
         out_shape=[
-            jax.ShapeDtypeStruct((fine_chunks, shares, fine, fan_out), jnp.bfloat16),
-            jax.ShapeDtypeStruct((coarse_chunks, coarse, fan_out), jnp.bfloat16),
+            jax.ShapeDtypeStruct((fine_chunks, shares, fine_rows, 128), jnp.bfloat16),
+            jax.ShapeDtypeStruct((coarse_chunks, coarse_rows, 128), jnp.bfloat16),
             jax.ShapeDtypeStruct((2, images, channels, width), jnp.bfloat16),
         ],
         in_specs=[vmem] + [any_space] * 7,
         out_specs=[vmem, vmem, any_space],
         scratch_shapes=Renewal.scratch(fine_chunks, fine, fan_out)
         + Renewal.scratch(coarse_chunks, coarse, fan_out)
-        + [pltpu.VMEM((fine_chunks, fine, fan_out), jnp.bfloat16)]
-        + Stream.scratch(fine_chunks, fine, fan_out, groups)
+        + [pltpu.VMEM((fine_chunks, fine_rows, 128), jnp.bfloat16)]
+        + Stream.scratch(fine_chunks, fine_rows, 128, groups)
         + [pltpu.SemaphoreType.DMA((2, 2, 1))],
         compiler_params=pltpu.CompilerParams(
             collective_id=0, has_side_effects=True, vmem_limit_bytes=56 << 20
         ),
     )(mask, *cut(fine_chunks), *cut(coarse_chunks), x)
-    return kernel.reshape(depth, fan_out), col, rims
+    return kernel, col, rims
 
 
 def silu(v):
@@ -387,7 +426,7 @@
 
 
 def first_kernel(groups, dp, x_ref, top_ref, bottom_ref, k_ref, col_ref, o_ref, out_ref, rims_ref,
-                 patch, wide, borders, edge_sem, *scratch):
+                 patch, wide, natural, borders, edge_sem, *scratch):
     place = Place(groups, dp)
     image, images = pl.program_id(0), pl.num_programs(0)
     height = x_ref.shape[1]
@@ -400,7 +439,8 @@
     @pl.when(image == 0)
     def _():
         place.meet()
-        wide[...] = k_ref[...].astype(jnp.float32).T.astype(jnp.bfloat16)
+        unpack(k_ref, natural)
+        wide[...] = natural[...].T.astype(jnp.bfloat16)
 
     def step(t, carry=0):
         at_step(t, coarse_chunks, lambda k: stream.to_col(k).start())
@@ -421,10 +461,11 @@
         each(count, edges.drain)
 
 
-def second_kernel(x_ref, top_ref, bottom_ref, k_ref, o_ref, patch, wide):
+def second_kernel(x_ref, top_ref, bottom_ref, k_ref, o_ref, patch, wide, natural):
     @pl.when(pl.program_id(0) == 0)
     def _():
-        wide[...] = k_ref[...].astype(jnp.float32).T.astype(jnp.bfloat16)
+        unpack(k_ref, natural)
+        wide[...] = natural[...].T.astype(jnp.bfloat16)
 
     conv_image(x_ref.at[0], top_ref.at[0, 0], bottom_ref.at[0, 0], o_ref.at[0], patch, wide)
 
@@ -436,9 +477,11 @@
     bottom = pl.BlockSpec((1, 1, channels, width), lambda i: (1, i, 0, 0))
     scratch = [
         pltpu.VMEM((height + 2, 3 * channels, width), jnp.bfloat16),
-        pltpu.VMEM(kernel.shape[::-1], jnp.bfloat16),
+        pltpu.VMEM((channels, 9 * channels), jnp.bfloat16),
+        pltpu.VMEM((9 * channels, channels), jnp.float32),
     ]
-    return image, [image, top, bottom, pl.BlockSpec(kernel.shape, lambda i: (0, 0))], scratch
+    whole = pl.BlockSpec(kernel.shape, lambda i: (0, 0, 0, 0))
+    return image, [image, top, bottom, whole], scratch
 
 
 def first_conv(x, rims, kernel, col):
@@ -467,7 +510,7 @@
             collective_id=1, has_side_effects=True, vmem_limit_bytes=56 << 20
         ),
     )(x, rims, rims, kernel, col)
-    return hidden, second.reshape(kernel.shape), rims
+    return hidden, second, rims
 
 
 def second_conv(x, rims, kernel):

time: 122 us -> 116 us (0.951)
  Pallas kernels: 120 us -> 114 us
    pallas_call x1, Pallas kernels: 49.9 us -> 46.1 us  [first_conv(): pl.pallas_call(functools.partial(first_kernel, groups, dp), out_shape=[ja...]
    pallas_call x1, Pallas kernels: 47 us -> 44.9 us  [spread(): pl.pallas_call(functools.partial(spread_kernel, groups, dp), out_shape=[j...]
where the time goes in v4:
time: 116 us
  Pallas kernels  114 us (98%)
    pallas_call x1, Pallas kernels, first_conv(): pl.pallas_call(functools.partial(first_kernel, groups, dp), out_shape=[ja...  46.1 us
    pallas_call x1, Pallas kernels, spread(): pl.pallas_call(functools.partial(spread_kernel, groups, dp), out_shape=[j...  44.9 us
    pallas_call x1, Pallas kernels, second_conv(): pl.pallas_call(second_kernel, out_shape=jax.ShapeDtypeStruct(x.shape, x.d...  23.4 us

profile of v4, /device:TPU:1, one launch (start us, length us, event | category | flops | bytes accessed | tf_op | source)
XLA Modules:
  0.0 115.7 jit_solution(646003694288951056)
XLA Ops:
  0.0 0.7 compare_convert_fusion
  0.7 0.7 broadcast_in_dim.2.mask_ref
  1.3 44.9 %shard_map.55 = (bf16[15,4,120,128]{3,2,1,0:T(8,128)(2,1)}, bf16[3,600,128]{2,1,0:T(8,128)(2,1)}, bf16[2,8,320,128]{3,2,1,0:T(8,128)(2,1)}) custom-call(f32[2,1,320]{2,1,0:T(1,128)} %broadcast_in_dim.2.mask_ref, bf16[30,4,48,320]{3,2,1,0:T(8,128)(2,1)} %bitcast.12, f32[30,4,48,320]{3,2,1,0:T(8,128)} %bitcast.8, bf16[30,4,48,320]{3,2,1,0:T(8,128)(2,1)} %bitcast.14, ...), custom_call_target="tpu_custom_call" | custom-call | tf_op jit(solution)/shard_map/pallas_call | solution.py:367
  46.2 46.1 %shard_map.56 = (bf16[8,8,320,128]{3,2,1,0:T(8,128)(2,1)}, bf16[3,4,600,128]{3,2,1,0:T(8,128)(2,1)}, bf16[2,8,320,128]{3,2,1,0:T(8,128)(2,1)}) custom-call(bf16[8,8,320,128]{3,2,1,0:T(8,128)(2,1)} %bitcast.11, bf16[2,8,320,128]{3,2,1,0:T(8,128)(2,1)} %get-tuple-element.11.top_ref.bottom_ref, bf16[2,8,320,128]{3,2,1,0:T(8,128)(2,1)} %get-tuple-element.11.top_ref.bottom_ref, ...), custom_call_target="tpu_custom_call" | custom-call | tf_op jit(solution)/shard_map/pallas_call | solution.py:493
  92.3 23.4 %shard_map.57 = bf16[8,8,320,128]{3,2,1,0:T(8,128)(2,1)} custom-call(bf16[8,8,320,128]{3,2,1,0:T(8,128)(2,1)} %get-tuple-element.14.x_ref, bf16[2,8,320,128]{3,2,1,0:T(8,128)(2,1)} %get-tuple-element.15.top_ref.bottom_ref, bf16[2,8,320,128]{3,2,1,0:T(8,128)(2,1)} %get-tuple-element.15.top_ref.bottom_ref, bf16[3,4,600,128]{3,2,1,0:T(8,128)(2,1)} %get-tuple-element.16.k_ref), custom_call_target="tpu_custom_call" | custom-call | tf_op jit(solution)/shard_map/pallas_call | solution.py:518

commit v5 on v4

--- a/solution.py
+++ b/solution.py
@@ -11,9 +11,10 @@
 learn_rate = 0.5
 MESH = pl.DeviceIdType.MESH
 fine_chunks = 15
-coarse_chunks = 3
-pair_hop = 3
-hop = 4
+coarse_chunks = 9
+pair_hop = 2
+hop = 3
+slow_hop = 4
 
 
 class Place:
@@ -337,7 +338,8 @@
         at_step(late - 1 - pair_hop, coarse_chunks, two.join)
         return carry
 
-    lax.fori_loop(0, pair_hop + stream.steps(fine_chunks, hop), step, 0)
+    ends = (pair_hop + stream.steps(fine_chunks, hop), fine_chunks + coarse_chunks + 2 * pair_hop + 1)
+    lax.fori_loop(0, max(ends), step, 0)
 
     def drain(k):
         one.to_pair(k).wait_send()
@@ -389,7 +391,7 @@
     return v / (1.0 + jnp.exp(-v))
 
 
-def conv_image(x_ref, top_ref, bottom_ref, o_ref, patch, wide):
+def conv_image(x_ref, top_ref, bottom_ref, o_ref, patch, wide, between=lambda row: None):
     height, channels, width = x_ref.shape
     at = lax.axis_index("dp")
     column = lax.broadcasted_iota(jnp.int32, (1, width), 1)
@@ -409,6 +411,7 @@
 
     built = 0
     for row in range(0, height, 2):
+        between(row)
         while built < row + 4:
             build(built)
             built += 1
@@ -444,11 +447,16 @@
 
     def step(t, carry=0):
         at_step(t, coarse_chunks, lambda k: stream.to_col(k).start())
-        stream.step(t, coarse_chunks, 1)
+        stream.step(t, coarse_chunks, slow_hop)
         return carry
 
-    step(image)
-    conv_image(x_ref.at[0], top_ref.at[0, 0], bottom_ref.at[0, 0], o_ref.at[0], patch, wide)
+    def between(row):
+        if row % (height // 2) == 0:
+            now = 4 * image + row // (height // 2) * 2
+            step(now)
+            step(now + 1)
+
+    conv_image(x_ref.at[0], top_ref.at[0, 0], bottom_ref.at[0, 0], o_ref.at[0], patch, wide, between)
     borders[image, 0] = o_ref[0, 0]
     borders[image, 1] = o_ref[0, height - 1]
     edges.start(image)
@@ -456,7 +464,7 @@
     @pl.when(image == images - 1)
     def _():
         count = borders.shape[0]
-        lax.fori_loop(count, max(count, stream.steps(coarse_chunks, 1)), step, 0)
+        lax.fori_loop(4 * count, max(4 * count, stream.steps(coarse_chunks, slow_hop)), step, 0)
         each(coarse_chunks, stream.drain)
         each(count, edges.drain)
 

time: 116 us -> 114 us (0.983)
    pallas_call x1, Pallas kernels: 46.1 us -> 43.4 us  [first_conv(): pl.pallas_call(functools.partial(first_kernel, groups, dp), out_shape=[ja...]
where the time goes in v5:
time: 114 us
  Pallas kernels  113 us (99%)
    pallas_call x1, Pallas kernels, spread(): pl.pallas_call(functools.partial(spread_kernel, groups, dp), out_shape=[j...  45.9 us
    pallas_call x1, Pallas kernels, first_conv(): pl.pallas_call(functools.partial(first_kernel, groups, dp), out_shape=[ja...  43.4 us
    pallas_call x1, Pallas kernels, second_conv(): pl.pallas_call(second_kernel, out_shape=jax.ShapeDtypeStruct(x.shape, x.d...  23.4 us

profile of v5, /device:TPU:1, one launch (start us, length us, event | category | flops | bytes accessed | tf_op | source)
XLA Modules:
  0.0 114.1 jit_solution(16567289108769379293)
XLA Ops:
  0.0 0.7 compare_convert_fusion
  0.7 0.7 broadcast_in_dim.2.mask_ref
  1.3 45.9 %shard_map.55 = (bf16[15,4,120,128]{3,2,1,0:T(8,128)(2,1)}, bf16[9,200,128]{2,1,0:T(8,128)(2,1)}, bf16[2,8,320,128]{3,2,1,0:T(8,128)(2,1)}) custom-call(f32[2,1,320]{2,1,0:T(1,128)} %broadcast_in_dim.2.mask_ref, bf16[30,4,48,320]{3,2,1,0:T(8,128)(2,1)} %bitcast.12, f32[30,4,48,320]{3,2,1,0:T(8,128)} %bitcast.8, bf16[30,4,48,320]{3,2,1,0:T(8,128)(2,1)} %bitcast.14, ...), custom_call_target="tpu_custom_call" | custom-call | tf_op jit(solution)/shard_map/pallas_call | solution.py:369
  47.2 43.4 %shard_map.56 = (bf16[8,8,320,128]{3,2,1,0:T(8,128)(2,1)}, bf16[9,4,200,128]{3,2,1,0:T(8,128)(2,1)}, bf16[2,8,320,128]{3,2,1,0:T(8,128)(2,1)}) custom-call(bf16[8,8,320,128]{3,2,1,0:T(8,128)(2,1)} %bitcast.11, bf16[2,8,320,128]{3,2,1,0:T(8,128)(2,1)} %get-tuple-element.11.top_ref.bottom_ref, bf16[2,8,320,128]{3,2,1,0:T(8,128)(2,1)} %get-tuple-element.11.top_ref.bottom_ref, ...), custom_call_target="tpu_custom_call" | custom-call | tf_op jit(solution)/shard_map/pallas_call | solution.py:501
  90.7 23.4 %shard_map.57 = bf16[8,8,320,128]{3,2,1,0:T(8,128)(2,1)} custom-call(bf16[8,8,320,128]{3,2,1,0:T(8,128)(2,1)} %get-tuple-element.14.x_ref, bf16[2,8,320,128]{3,2,1,0:T(8,128)(2,1)} %get-tuple-element.15.top_ref.bottom_ref, bf16[2,8,320,128]{3,2,1,0:T(8,128)(2,1)} %get-tuple-element.15.top_ref.bottom_ref, bf16[9,4,200,128]{3,2,1,0:T(8,128)(2,1)} %get-tuple-element.16.k_ref), custom_call_target="tpu_custom_call" | custom-call | tf_op jit(solution)/shard_map/pallas_call | solution.py:526
